TPU v7x, 32 devices: a whole 2x2x4 slice. The times are simulated.
32 devices in a mesh: tile: 4 (over y, x), orient: 8 (over z, core).
Axes of the slice: x: 2, y: 2, z: 4, core: 2. Of those that a mesh axis runs over, the one named last changes fastest.
Arguments:
- micrograph_tiles: bfloat16 [8, 512, 512], P('tile'), as said below
- tile_offsets: int32 [8, 2], P('tile'), may hold values from 0 to 3584
- library: bfloat16 [32, 8, 128, 128], P('tile', 'orient'), as said below
- orient_ids: int32 [8, 2], P('orient'), may hold values from 0 to 31
Outputs:
- peak_score: float32 [8, 384, 384], P('tile')
- z_score: float32 [8, 384, 384], P('tile')
Inputs may be any that keep to these rules, and one draw needn't show every extreme that they name: `micrograph_tiles`: real-valued pixel intensities of the tiles. `library`: real-valued projection densities.
All inputs are finite; a program needn't handle non-finite values.
Results may differ from a plain program's by a relative error of at most 0.0095.
Values may be sent and summed in bfloat16 or wider, within the bound.
A program may use at most 64 MiB of HBM per device.

v0:
```python
import functools
import math

import jax
import jax.numpy as jnp
import numpy as np
from jax import lax
from jax.experimental import pallas as pl
from jax.experimental.pallas import tpu as pltpu
from jax.sharding import PartitionSpec as P

VALID = 384

AMPLITUDE = 0.07
DEFOCUS_BASE = 100.0
DEFOCUS_TILT = 0.002
FLOOR_SHARE = 0.25
MESH = pl.DeviceIdType.MESH
VMEM = pl.BlockSpec(memory_space=pltpu.VMEM)
SMEM = pl.BlockSpec(memory_space=pltpu.SMEM)
GRANT = 56 * 1024 * 1024


def tables(length, valid):
    half = length // 2
    rows = -(-(half + 1) // 16) * 16
    a_index = np.concatenate([np.arange(0, length, 2), np.arange(1, length, 2)])
    j_index = np.arange(length)
    b_index = np.arange(half + 1)

    def wave(function, left, right):
        return function((left[:, None] * right[None, :]) % length * (2.0 * np.pi / length))

    first = np.zeros((2, rows, length))
    first[0, : half + 1] = wave(np.cos, b_index, j_index)
    first[1, : half + 1] = -wave(np.sin, b_index, j_index)
    second_cos = wave(np.cos, j_index, a_index)
    second_sin = wave(np.sin, j_index, a_index)
    back = []
    for parity in range(2):
        cosine = wave(np.cos, a_index[parity * half : (parity + 1) * half], j_index[:half])
        sine = wave(np.sin, a_index[parity * half : (parity + 1) * half], j_index[:half])
        back.append(np.block([[cosine, sine], [-sine, cosine]]))
    count = np.full((half,), 2.0)
    count[0] = 1.0
    last_cos = wave(np.cos, j_index[:valid], b_index[:half]) * count / length
    last_sin = -wave(np.sin, j_index[:valid], b_index[:half]) * count / length
    last_sin[:, 0] = np.cos(np.pi * j_index[:valid]) / length
    last = np.concatenate([last_cos, last_sin], axis=1)

    signed = np.where(a_index < half, a_index, a_index - length) / length
    a_square = (signed * signed)[None, :]
    b_square = np.zeros((rows, 1))
    b_square[: half + 1, 0] = (b_index / length) ** 2
    weight = np.zeros((rows, 1))
    weight[: half + 1, 0] = 2.0
    weight[0, 0] = weight[half, 0] = 1.0

    def narrow(value):
        return np.asarray(value, np.float32).astype(jnp.bfloat16)

    return dict(
        first=narrow(first.reshape(2 * rows, length)),
        cos=narrow(second_cos),
        sin=narrow(second_sin),
        even=narrow(back[0]),
        odd=narrow(back[1]),
        last=narrow(last),
        a_square=a_square.astype(np.float32),
        b_square=b_square.astype(np.float32),
        weight=weight.astype(np.float32),
    )


def dot(left, right):
    return jnp.dot(left, right, preferred_element_type=jnp.float32)


def dot_nt(left, right):
    return lax.dot_general(
        left, right, (((1,), (1,)), ((), ())), preferred_element_type=jnp.float32
    )


def sine_of_turns(turns):
    part = turns - jnp.floor(turns + 0.5)
    mirrored = jnp.where(part > 0.0, 0.5, -0.5) - part
    part = jnp.where(jnp.abs(part) > 0.25, mirrored, part)
    angle = part * (2.0 * math.pi)
    square = angle * angle
    poly = -1.0 / 39916800.0
    for term in (1.0 / 362880.0, -1.0 / 5040.0, 1.0 / 120.0, -1.0 / 6.0, 1.0):
        poly = poly * square + term
    return angle * poly


def forward_kernel(
    ids_ref, off_ref, x_ref, lib_ref, first_ref, cos_ref, sin_ref, a_ref, b_ref,
    real_ref, imag_ref, con_ref, pow_ref, tpl_ref,
):
    core = lax.rem(lax.axis_index("orient"), 2)
    mine = lax.axis_index("tile")
    slots = lib_ref.shape[0]
    rows, length = real_ref.shape
    half = length // 2
    for step in range(tpl_ref.shape[0]):
        chosen = ids_ref[0, step]
        owner = chosen // slots
        picked = lib_ref[chosen - owner * slots, 0]
        keep = jnp.where(owner == mine, 1.0, 0.0).astype(jnp.float32)
        tpl_ref[step] = jnp.where(keep > 0.0, picked.astype(jnp.float32), 0.0).astype(jnp.bfloat16)
    halves = dot_nt(first_ref[...], x_ref[core]).astype(jnp.bfloat16)
    half_real, half_imag = halves[:rows], halves[rows:]
    spec_real = dot(half_real, cos_ref[...]) + dot(half_imag, sin_ref[...])
    spec_imag = dot(half_imag, cos_ref[...]) - dot(half_real, sin_ref[...])
    power = spec_real * spec_real + spec_imag * spec_imag
    pow_ref[0] = power[:, :half].astype(jnp.bfloat16)
    pow_ref[1] = power[:, half:].astype(jnp.bfloat16)
    s2 = a_ref[...] + b_ref[...]
    tilt = (off_ref[core, 0] - off_ref[core, 1]).astype(jnp.float32)
    defocus = DEFOCUS_BASE + DEFOCUS_TILT * tilt
    shift = math.asin(AMPLITUDE) / (2.0 * math.pi)
    contrast = -sine_of_turns(s2 * (0.5 * defocus) + shift)
    contrast = jnp.where(s2 > 0.0, contrast, 0.0)
    con_ref[...] = contrast
    real_ref[...] = spec_real * contrast
    imag_ref[...] = spec_imag * contrast


def exchange_kernel(
    n_tile, n_orient, pow_ref, tpl_ref, total_ref, all_ref,
    pair_in, half_out, half_in, done_out, done_in, tpl_in, held, send_sem, recv_sem,
):
    tile = lax.axis_index("tile")
    orient = lax.axis_index("orient")
    core = lax.rem(orient, 2)
    chip = orient // 2
    n_chip = n_orient // 2
    partner = (tile, chip * 2 + 1 - core)
    tiles = [(lax.rem(tile + k, n_tile), orient) for k in range(1, n_tile)]
    chips = [(tile, lax.rem(chip + k, n_chip) * 2 + core) for k in range(1, n_chip)]

    barrier = pltpu.get_barrier_semaphore()
    for device in [partner] + tiles + chips:
        pl.semaphore_signal(barrier, inc=1, device_id=device, device_id_type=MESH)
    pl.semaphore_wait(barrier, 1 + len(tiles) + len(chips))

    used = [0]

    def send(src, dst, device):
        at = used[0]
        used[0] += 1
        copy = pltpu.make_async_remote_copy(
            src_ref=src, dst_ref=dst, send_sem=send_sem.at[at], recv_sem=recv_sem.at[at],
            device_id=device, device_id_type=MESH,
        )
        copy.start()
        return copy

    pair = send(pow_ref.at[1 - core], pair_in, partner)
    picks = [send(tpl_ref, tpl_in.at[k], device) for k, device in enumerate(tiles)]
    pair.wait()
    mine = pow_ref[core].astype(jnp.float32) + pair_in[...].astype(jnp.float32)
    half_out[...] = mine.astype(jnp.bfloat16)
    sums = [send(half_out, half_in.at[k], device) for k, device in enumerate(tiles)]
    template = tpl_ref[...].astype(jnp.float32)
    for k, copy in enumerate(picks):
        copy.wait()
        template = template + tpl_in[k].astype(jnp.float32)
    held[core, chip] = template.astype(jnp.bfloat16)
    spread = [send(held.at[core, chip], held.at[core, chip], device) for device in chips]
    for copy in sums:
        copy.wait()
    total = half_out[...].astype(jnp.float32)
    for k in range(len(tiles)):
        total = total + half_in[k].astype(jnp.float32)
    done_out[...] = total
    last = send(done_out, done_in, partner)
    for copy in spread:
        copy.wait()
    swap = send(held.at[core], held.at[core], partner)
    total_ref[core] = total
    last.wait()
    total_ref[1 - core] = done_in[...]
    swap.wait()
    all_ref[...] = held[...]


def search_kernel(
    tiles, real_ref, imag_ref, con_ref, total_ref, tpl_ref, first_ref, cos_ref, sin_ref,
    even_ref, odd_ref, last_ref, weight_ref, out_ref,
    g_real, g_imag, g_energy, base_table, mids, peak, total_sum, squares,
):
    rows, length = real_ref.shape
    half = length // 2
    valid = last_ref.shape[0]
    groups, steps, size, _ = tpl_ref.shape
    weight = weight_ref[...]
    sides = [total_ref[side] / tiles for side in range(2)]
    mean = (jnp.sum(sides[0] * weight) + jnp.sum(sides[1] * weight)) / (length * length)
    floor = FLOOR_SHARE * mean
    for side in range(2):
        columns = slice(side * half, (side + 1) * half)
        whiten2 = 1.0 / jnp.maximum(sides[side], floor)
        contrast = con_ref[:, columns]
        g_real[:, columns] = (real_ref[:, columns] * whiten2).astype(jnp.bfloat16)
        g_imag[:, columns] = (imag_ref[:, columns] * whiten2).astype(jnp.bfloat16)
        g_energy[:, columns] = contrast * contrast * whiten2 * (weight / (length * length))
    base_table[:size, :length] = cos_ref[:size]
    base_table[:size, length:] = -sin_ref[:size]
    base_table[size:, :length] = sin_ref[:size]
    base_table[size:, length:] = cos_ref[:size]
    peak[...] = jnp.full_like(peak, -jnp.inf)
    total_sum[...] = jnp.zeros_like(total_sum)
    squares[...] = jnp.zeros_like(squares)

    def visit(group, carry):
        images = tpl_ref[group].reshape(steps * size, size)
        halves = dot_nt(first_ref[...], images).astype(jnp.bfloat16)
        scales = []
        for step in range(steps):
            columns = slice(step * size, (step + 1) * size)
            joined = jnp.concatenate([halves[:rows, columns], halves[rows:, columns]], axis=1)
            base = dot(joined, base_table[...])
            base_real, base_imag = base[:, :length], base[:, length:]
            energy = jnp.sum(g_energy[...] * (base_real * base_real + base_imag * base_imag))
            scales.append(lax.rsqrt(energy + 1e-06))
            short_real, short_imag = base_real.astype(jnp.bfloat16), base_imag.astype(jnp.bfloat16)
            prod_real = g_real[...] * short_real + g_imag[...] * short_imag
            prod_imag = g_imag[...] * short_real - g_real[...] * short_imag
            even = dot(
                jnp.concatenate([prod_real[:, :half], prod_imag[:, :half]], axis=1), even_ref[...]
            )
            odd = dot(
                jnp.concatenate([prod_real[:, half:], prod_imag[:, half:]], axis=1), odd_ref[...]
            )
            both, apart = even + odd, even - odd
            mid_real = jnp.concatenate([both[:, :half], apart[:, : valid - half]], axis=1)
            mid_imag = jnp.concatenate([both[:half, half:], apart[:half, half:valid]], axis=1)
            row = lax.broadcasted_iota(jnp.int32, (half, valid), 0)
            mid_imag = jnp.where(row == 0, mid_real[half : half + 1], mid_imag)
            place = slice(step * valid, (step + 1) * valid)
            mids[:half, place] = mid_real[:half].astype(jnp.bfloat16)
            mids[half:, place] = mid_imag.astype(jnp.bfloat16)
        found = dot(last_ref[...], mids[...])
        top, add, add2 = peak[...], total_sum[...], squares[...]
        for step in range(steps):
            score = found[:, step * valid : (step + 1) * valid] * scales[step]
            top = jnp.maximum(top, score)
            add = add + score
            add2 = add2 + score * score
        peak[...] = top
        total_sum[...] = add
        squares[...] = add2
        return carry

    lax.fori_loop(0, groups, visit, 0)
    searched = groups * steps
    mean_score = total_sum[...] / searched
    variance = squares[...] / searched - mean_score * mean_score
    z_score = (peak[...] - mean_score) * lax.rsqrt(variance + 1e-06)
    out_ref[0] = peak[...].T.astype(jnp.bfloat16)
    out_ref[1] = z_score.T.astype(jnp.bfloat16)


def swap_kernel(in_ref, out_ref, held, send_sem, recv_sem):
    tile = lax.axis_index("tile")
    orient = lax.axis_index("orient")
    core = lax.rem(orient, 2)
    partner = (tile, (orient // 2) * 2 + 1 - core)
    barrier = pltpu.get_barrier_semaphore()
    pl.semaphore_signal(barrier, inc=1, device_id=partner, device_id_type=MESH)
    pl.semaphore_wait(barrier, 1)
    copy = pltpu.make_async_remote_copy(
        src_ref=in_ref, dst_ref=held, send_sem=send_sem, recv_sem=recv_sem,
        device_id=partner, device_id_type=MESH,
    )
    copy.start()
    for which in range(2):
        out_ref[which, core] = in_ref[which]
    copy.wait()
    for which in range(2):
        out_ref[which, 1 - core] = held[which]


def body(n_tile, n_orient, micrograph_tiles, tile_offsets, library, orient_ids):
    tile_count, length = micrograph_tiles.shape[:2]
    slots, _, size, _ = library.shape
    steps = orient_ids.shape[1]
    n_chip = n_orient // 2
    assert tile_count == 2 and n_orient % 2 == 0
    half = length // 2
    t = tables(length, VALID)
    rows = t["weight"].shape[0]
    f32, bf16 = jnp.float32, jnp.bfloat16
    shape = jax.ShapeDtypeStruct
    plane = shape((rows, length), f32)
    params = pltpu.CompilerParams(vmem_limit_bytes=GRANT)

    real, imag, contrast, power, picked = pl.pallas_call(
        forward_kernel,
        out_shape=(plane, plane, plane, shape((2, rows, half), bf16), shape((steps, size, size), bf16)),
        in_specs=[SMEM, SMEM] + [VMEM] * 7,
        out_specs=(VMEM,) * 5,
        compiler_params=params,
    )(
        orient_ids, tile_offsets, micrograph_tiles, library, t["first"], t["cos"], t["sin"],
        t["a_square"], t["b_square"],
    )

    copies = 3 + 2 * (n_tile - 1) + (n_chip - 1)
    total, templates = pl.pallas_call(
        functools.partial(exchange_kernel, n_tile, n_orient),
        out_shape=(shape((2, rows, half), f32), shape((2, n_chip, steps, size, size), bf16)),
        in_specs=[VMEM] * 2,
        out_specs=(VMEM,) * 2,
        scratch_shapes=[
            pltpu.VMEM((rows, half), bf16),
            pltpu.VMEM((rows, half), bf16),
            pltpu.VMEM((n_tile - 1, rows, half), bf16),
            pltpu.VMEM((rows, half), f32),
            pltpu.VMEM((rows, half), f32),
            pltpu.VMEM((n_tile - 1, steps, size, size), bf16),
            pltpu.VMEM((2, n_chip, steps, size, size), bf16),
            pltpu.SemaphoreType.DMA((copies,)),
            pltpu.SemaphoreType.DMA((copies,)),
        ],
        compiler_params=pltpu.CompilerParams(collective_id=0, has_side_effects=True),
    )(power, picked)

    found = pl.pallas_call(
        functools.partial(search_kernel, tile_count * n_tile),
        out_shape=shape((2, VALID, VALID), bf16),
        in_specs=[VMEM] * 12,
        out_specs=VMEM,
        scratch_shapes=[
            pltpu.VMEM((rows, length), bf16),
            pltpu.VMEM((rows, length), bf16),
            pltpu.VMEM((rows, length), f32),
            pltpu.VMEM((2 * size, 2 * length), bf16),
            pltpu.VMEM((length, steps * VALID), bf16),
            pltpu.VMEM((VALID, VALID), f32),
            pltpu.VMEM((VALID, VALID), f32),
            pltpu.VMEM((VALID, VALID), f32),
        ],
        compiler_params=params,
    )(
        real, imag, contrast, total, templates.reshape(n_orient, steps, size, size),
        np.ascontiguousarray(t["first"][:, :size]), t["cos"], t["sin"], t["even"], t["odd"],
        t["last"], t["weight"],
    )

    both = pl.pallas_call(
        swap_kernel,
        out_shape=shape((2, 2, VALID, VALID), bf16),
        in_specs=[VMEM],
        out_specs=VMEM,
        scratch_shapes=[
            pltpu.VMEM((2, VALID, VALID), bf16),
            pltpu.SemaphoreType.DMA,
            pltpu.SemaphoreType.DMA,
        ],
        compiler_params=pltpu.CompilerParams(collective_id=1, has_side_effects=True),
    )(found)
    return (both[0].astype(f32), both[1].astype(f32))


def solution(mesh):
    placed = (
        P("tile", None, None),
        P("tile", None),
        P("tile", "orient", None, None),
        P("orient", None),
    )
    return jax.shard_map(
        functools.partial(body, mesh.shape["tile"], mesh.shape["orient"]),
        mesh=mesh,
        in_specs=placed,
        out_specs=(P("tile", None, None), P("tile", None, None)),
        check_vma=False,
    )
```

profile of v0, /device:TPU:0, one launch (start us, length us, event | category | flops | bytes accessed | tf_op | source)
XLA Modules:
  0.0 50.3 jit_solution(7557509242857608188)
XLA Ops:
  0.6 4.4 %shard_map.149 = (f32[272,512]{1,0:T(8,128)}, f32[272,512]{1,0:T(8,128)}, f32[272,512]{1,0:T(8,128)}, bf16[2,272,256]{2,1,0:T(8,128)(2,1)}, bf16[2,128,128]{2,1,0:T(8,128)(2,1)}) custom-call(s32[1,2]{1,0:T(1,128)} %ids_ref.1, s32[2,2]{1,0:T(2,128)} %off_ref.1, bf16[2,512,512]{2,1,0:T(8,128)(2,1)} %x_ref.1, bf16[8,1,128,128]{3,2,1,0:T(8,128)(2,1)} %lib_ref.1, ...), custom_call_target="tpu_custom_call" | custom-call | tf_op jit(solution)/shard_map/pallas_call | solution.py:300
  5.0 19.8 %shard_map.150 = (f32[2,272,256]{2,1,0:T(8,128)}, bf16[2,4,2,128,128]{4,3,2,1,0:T(8,128)(2,1)}) custom-call(bf16[2,272,256]{2,1,0:T(8,128)(2,1)} %get-tuple-element.12.pow_ref, bf16[2,128,128]{2,1,0:T(8,128)(2,1)} %get-tuple-element.13.tpl_ref), custom_call_target="tpu_custom_call" | custom-call | tf_op jit(solution)/shard_map/pallas_call | solution.py:312
  24.9 18.5 %shard_map.151.in_ref = bf16[2,384,384]{2,1,0:T(8,128)(2,1)} custom-call(f32[272,512]{1,0:T(8,128)} %get-tuple-element.9.real_ref, f32[272,512]{1,0:T(8,128)} %get-tuple-element.10.imag_ref, f32[272,512]{1,0:T(8,128)} %get-tuple-element.11.con_ref, f32[2,272,256]{2,1,0:T(8,128)} %get-tuple-element.14.total_ref, bf16[8,2,128,128]{3,2,1,0:T(8,128)(2,1)} %bitcast.7, ...), custom_call_target="tpu_custom_call" | custom-call | tf_op jit(solution)/shard_map/pallas_call | solution.py:331
  43.4 4.2 %shard_map.152 = bf16[2,2,384,384]{3,2,1,0:T(8,128)(2,1)} custom-call(bf16[2,384,384]{2,1,0:T(8,128)(2,1)} %shard_map.151.in_ref), custom_call_target="tpu_custom_call" | custom-call | tf_op jit(solution)/shard_map/pallas_call | solution.py:353
  47.5 2.8 %bitcast_convert_fusion = (f32[2,384,384]{2,1,0:T(8,128)}, f32[2,384,384]{2,1,0:T(8,128)}) fusion(bf16[2,2,384,384]{3,2,1,0:T(8,128)(2,1)} %shard_map.152), kind=kLoop, calls=%fused_computation | loop fusion | flops 589824 | bytes 3538944 | tf_op jit(solution)/shard_map/convert_element_type | solution.py:365
where the time goes:
time: 50.6 us; the launch traced here: 50.3 us
  Pallas kernels  46.9 us (93%)
  other arithmetic  2.8 us (6%)
  between operations  0.65 us (1%)
    pallas_call x1, Pallas kernels, body(): pl.pallas_call(functools.partial(exchange_kernel, n_tile, n_orient), out_...  19.8 us
    pallas_call x1, Pallas kernels, body(): pl.pallas_call(functools.partial(search_kernel, tile_count * n_tile), out...  18.5 us
    pallas_call x1, Pallas kernels, body(): pl.pallas_call(forward_kernel, out_shape=(plane, plane, plane, shape((2,...  4.4 us
    pallas_call x1, Pallas kernels, body(): pl.pallas_call(swap_kernel, out_shape=shape((2, 2, VALID, VALID), bf16),...  4.16 us
    convert_element_type x1, other arithmetic, body(): return (both[0].astype(f32), both[1].astype(f32))  2.8 us

commit v1 on v0

v1 whole, which is shorter than its diff:
```python
import functools
import math

import jax
import jax.numpy as jnp
import numpy as np
from jax import lax
from jax.experimental import pallas as pl
from jax.experimental.pallas import tpu as pltpu
from jax.sharding import PartitionSpec as P

VALID = 384
AMPLITUDE = 0.07
DEFOCUS_BASE = 100.0
DEFOCUS_TILT = 0.002
FLOOR_SHARE = 0.25
f32, bf16 = jnp.float32, jnp.bfloat16
MESH = pl.DeviceIdType.MESH
VMEM = pl.BlockSpec(memory_space=pltpu.VMEM)
SMEM = pl.BlockSpec(memory_space=pltpu.SMEM)
ANY = pl.BlockSpec(memory_space=pl.ANY)
GRANT = 46 * 1024 * 1024


def tables(length, size, valid):
    half, quarter = length // 2, length // 4
    rows = -(-(half + 1) // 16) * 16
    b_index = np.concatenate([np.arange(0, half, 2), np.arange(1, half, 2), [half]])
    a_index = np.concatenate([np.arange(r, length, 4) for r in range(4)])
    j_index = np.arange(length)

    def wave(function, left, right):
        return function((left[:, None] * right[None, :]) % length * (2.0 * np.pi / length))

    first = np.zeros((2, rows, length))
    first[0, : half + 1] = wave(np.cos, b_index, j_index)
    first[1, : half + 1] = -wave(np.sin, b_index, j_index)
    cosine = wave(np.cos, j_index, a_index)
    sine = wave(np.sin, j_index, a_index)
    base, back = [], []
    for r in range(4):
        columns = slice(r * quarter, (r + 1) * quarter)
        c, s = cosine[:size, columns], sine[:size, columns]
        base.append((np.concatenate([c, s]), np.concatenate([-s, c])))
        c = wave(np.cos, a_index[columns], j_index[:quarter])
        s = wave(np.sin, a_index[columns], j_index[:quarter])
        back.append(np.block([[c, s], [-s, c]]))
    last = []
    for parity in range(2):
        b_part = b_index[parity * quarter : (parity + 1) * quarter]
        count = np.where(b_part == 0, 1.0, 2.0)
        c = wave(np.cos, j_index[:half], b_part) * count / length
        s = -wave(np.sin, j_index[:half], b_part) * count / length
        if parity == 0:
            s[:, 0] = np.cos(np.pi * j_index[:half]) / length
        last.append(np.concatenate([c, s], axis=1))

    def narrow(value):
        return np.asarray(value, np.float32).astype(jnp.bfloat16)

    first = first.reshape(2 * rows, length)
    return dict(
        first=narrow(first),
        small=narrow(np.ascontiguousarray(first[:, :size])),
        cos=narrow(cosine),
        sin=narrow(sine),
        base=narrow(np.concatenate([base[2 * p + q][w] for p in range(2) for w in range(2) for q in range(2)], axis=1)),
        back=narrow(np.stack(back)),
        last=narrow(np.stack(last)),
    )


def dot(left, right):
    return jnp.dot(left, right, preferred_element_type=jnp.float32)


def sine_of_turns(turns):
    part = turns - jnp.floor(turns + 0.5)
    mirrored = jnp.where(part > 0.0, 0.5, -0.5) - part
    part = jnp.where(jnp.abs(part) > 0.25, mirrored, part)
    angle = part * (2.0 * math.pi)
    square = angle * angle
    poly = -1.0 / 39916800.0
    for term in (1.0 / 362880.0, -1.0 / 5040.0, 1.0 / 120.0, -1.0 / 6.0, 1.0):
        poly = poly * square + term
    return angle * poly


def row_index(rows, half):
    row = lax.broadcasted_iota(jnp.int32, (rows, 1), 0)
    quarter = half // 2
    return row, jnp.where(row < quarter, 2 * row, jnp.where(row < half, 2 * row - half + 1, row))


def row_weight(rows, half):
    row, b_index = row_index(rows, half)
    single = (b_index == 0) | (row == half)
    return jnp.where(row > half, 0.0, jnp.where(single, 1.0, 2.0)).astype(f32)


def tile_contrast(tilt, con_ref):
    rows, length = con_ref.shape
    half, quarter = length // 2, length // 4
    row, b_index = row_index(rows, half)
    b_index = jnp.where(row > half, 0, b_index).astype(f32) / length
    lane = lax.broadcasted_iota(jnp.int32, (1, length), 1)
    a_index = 4 * lax.rem(lane, quarter) + lane // quarter
    a_index = jnp.where(a_index < half, a_index, a_index - length).astype(f32) / length
    s2 = a_index * a_index + b_index * b_index
    defocus = DEFOCUS_BASE + DEFOCUS_TILT * tilt
    shift = math.asin(AMPLITUDE) / (2.0 * math.pi)
    contrast = -sine_of_turns(s2 * (0.5 * defocus) + shift)
    con_ref[...] = jnp.where(s2 > 0.0, contrast, 0.0)


def template_spectra(images, small_ref, table_ref, base_ref, power_ref, place):
    rows = small_ref.shape[0] // 2
    size = images.shape[0]
    half = table_ref.shape[1] // 4
    halves = dot(small_ref[...], images).astype(bf16)
    for n in range(images.shape[1] // size):
        columns = slice(n * size, (n + 1) * size)
        joined = jnp.concatenate([halves[:rows, columns], halves[rows:, columns]], axis=1)
        for side in range(2):
            at = 2 * side * half
            real = dot(joined, table_ref[:, at : at + half])
            imag = dot(joined, table_ref[:, at + half : at + 2 * half])
            base_ref[place(n), :, at : at + half] = real.astype(bf16)
            base_ref[place(n), :, at + half : at + 2 * half] = imag.astype(bf16)
            power_ref[place(n), :, side * half : (side + 1) * half] = (real * real + imag * imag).astype(bf16)


def tile_gains(tiles, total_ref, real_ref, imag_ref, con_ref, g_real, g_imag, g_energy):
    rows, length = real_ref.shape
    half = length // 2
    weight = row_weight(rows, half)
    mean = (jnp.sum(total_ref[0] * weight) + jnp.sum(total_ref[1] * weight)) / tiles
    floor = FLOOR_SHARE * (mean / (length * length))
    for side in range(2):
        columns = slice(side * half, (side + 1) * half)
        whiten2 = 1.0 / jnp.maximum(total_ref[side] / tiles, floor)
        contrast = con_ref[:, columns]
        gain = contrast * whiten2
        g_real[:, columns] = (real_ref[:, columns] * gain).astype(bf16)
        g_imag[:, columns] = (imag_ref[:, columns] * gain).astype(bf16)
        g_energy[:, columns] = (contrast * gain * (weight / (length * length))).astype(bf16)


def energy(t, power_ref, g_energy, part_ref):
    rows, length = g_energy.shape
    share = power_ref[t] * g_energy[...]
    share = share[:, : length // 2] + share[:, length // 2 :]
    total = None
    for row in range(0, rows, 16):
        piece = share[row : row + 8] + share[row + 8 : row + 16]
        piece = piece.astype(f32)
        total = piece if total is None else total + piece
    part_ref[t] = total[:, : length // 4] + total[:, length // 4 :]


def half_back(t, column, base_ref, back_ref, g_real, g_imag, mids):
    rows, length = g_real.shape
    quarter = length // 4
    half = 2 * quarter
    found = []
    for side in range(2):
        columns = slice(side * half, (side + 1) * half)
        at = 2 * side * half
        base_real = base_ref[t, :, at : at + half]
        base_imag = base_ref[t, :, at + half : at + 2 * half]
        gain_real, gain_imag = g_real[:, columns], g_imag[:, columns]
        prod_real = gain_real * base_real + gain_imag * base_imag
        prod_imag = gain_imag * base_real - gain_real * base_imag
        for q in range(2):
            part = slice(q * quarter, (q + 1) * quarter)
            joined = jnp.concatenate([prod_real[:, part], prod_imag[:, part]], axis=1)
            found.append(dot(joined, back_ref[2 * side + q]))
    plus02, minus02 = found[0] + found[2], found[0] - found[2]
    plus13, minus13 = found[1] + found[3], found[1] - found[3]
    real, imag = slice(0, quarter), slice(quarter, 2 * quarter)
    out = (
        (plus02[:, real] + plus13[:, real], plus02[:, imag] + plus13[:, imag]),
        (minus02[:, real] - minus13[:, imag], minus02[:, imag] + minus13[:, real]),
        (plus02[:, real] - plus13[:, real], plus02[:, imag] - plus13[:, imag]),
    )
    row = lax.broadcasted_iota(jnp.int32, (quarter, quarter), 0)
    for k, (mid_real, mid_imag) in enumerate(out):
        top = jnp.where(row == 0, mid_real[2 * quarter : 2 * quarter + 1], mid_imag[:quarter])
        mids[k, 0:quarter, column] = mid_real[:quarter].astype(bf16)
        mids[k, quarter : 2 * quarter, column] = top.astype(bf16)
        mids[k, 2 * quarter : 3 * quarter, column] = mid_real[quarter : 2 * quarter].astype(bf16)
        mids[k, 3 * quarter : 4 * quarter, column] = mid_imag[quarter : 2 * quarter].astype(bf16)


def scales_of(part_ref, count):
    return [lax.rsqrt(jnp.sum(part_ref[t]) + 1e-06) for t in range(count)]


def statistics(k, n, fresh, scales, mids, last_ref, stat_ref):
    quarter = last_ref.shape[1] // 2
    half = 2 * quarter
    columns = slice(n * half, (n + 1) * half)
    even = dot(last_ref[0], mids[k, :half, columns])
    odd = dot(last_ref[1], mids[k, half:, columns])
    one, two = scales
    for rows, (e, o) in ((slice(0, half), (even, odd)), (slice(half, half + quarter), (even[:quarter], -odd[:quarter]))):
        left = (e[:, :quarter] + o[:, :quarter]) * one
        right = (e[:, quarter:] + o[:, quarter:]) * two
        top, add, square = jnp.maximum(left, right), left + right, left * left + right * right
        if not fresh:
            top = jnp.maximum(stat_ref[0, rows], top)
            add = stat_ref[1, rows] + add
            square = stat_ref[2, rows] + square
        stat_ref[0, rows] = top
        stat_ref[1, rows] = add
        stat_ref[2, rows] = square


def finish(stats, searched):
    peak, add, squares = stats
    mean = add / searched
    variance = squares / searched - mean * mean
    return peak, (peak - mean) * lax.rsqrt(variance + 1e-06)


def search_kernel(
    n_tile, n_orient, valid,
    ids_ref, off_ref, x_hbm, lib_hbm, first_hbm, cos_hbm, sin_hbm, small_hbm, table_hbm, back_hbm,
    last_hbm, out_ref,
    x_ref, lib_ref, first_ref, cos_ref, sin_ref, small_ref, table_ref, back_ref, last_ref,
    real_ref, imag_ref, con_ref, halves_ref, pow_ref, pair_ref, sum_out, sum_in, total_ref,
    picks, parts, held, g_real, g_imag, g_energy, base_ref, power_ref, part_ref, mids, stat_ref,
    local_sem, pick_send, pick_recv, spread_send, spread_recv, gather_send, gather_recv,
    swap_send, swap_recv, pair_send, pair_recv, sum_send, sum_recv, done_send, done_recv,
    out_send, out_recv,
):
    tile = lax.axis_index("tile")
    orient = lax.axis_index("orient")
    core = lax.rem(orient, 2)
    chip = orient // 2
    n_chip = n_orient // 2
    steps, size = picks.shape[1], picks.shape[3]
    slots = lib_ref.shape[0]
    rows, length = real_ref.shape
    half, quarter = length // 2, length // 4
    partner = (tile, chip * 2 + 1 - core)
    tiles = [(lax.rem(tile + k, n_tile), orient) for k in range(1, n_tile)]
    chips = [(tile, lax.rem(chip + k, n_chip) * 2 + core) for k in range(1, n_chip)]
    strides = [1 << s for s in range((n_tile - 1).bit_length())]

    def local(at, src, dst):
        copy = pltpu.make_async_copy(src, dst, local_sem.at[at])
        copy.start()
        return copy

    loads = dict(
        lib=local(0, lib_hbm, lib_ref),
        x=local(1, x_hbm.at[core], x_ref),
        first=local(2, first_hbm, first_ref),
        cos=local(3, cos_hbm, cos_ref),
        sin=local(4, sin_hbm, sin_ref),
        small=local(5, small_hbm, small_ref),
        table=local(6, table_hbm, table_ref),
        back=local(7, back_hbm, back_ref),
        last=local(8, last_hbm, last_ref),
    )
    barrier = pltpu.get_barrier_semaphore()
    for device in [partner] + tiles + chips:
        pl.semaphore_signal(barrier, inc=1, device_id=device, device_id_type=MESH)

    def send(src, dst, send_sem, recv_sem, device):
        copy = pltpu.make_async_remote_copy(
            src_ref=src, dst_ref=dst, send_sem=send_sem, recv_sem=recv_sem,
            device_id=device, device_id_type=MESH,
        )
        copy.start()
        return copy

    strip = size // n_tile
    loads["lib"].wait()
    for step in range(steps):
        chosen = ids_ref[0, step]
        owner = chosen // slots
        picked = lib_ref[chosen - owner * slots, 0]
        keep = jnp.where(owner == tile, 1.0, 0.0).astype(f32)
        picked = jnp.where(keep > 0.0, picked.astype(f32), 0.0).astype(bf16)
        for q in range(n_tile):
            picks[q, step] = picked[q * strip : (q + 1) * strip]
    pl.semaphore_wait(barrier, 1 + len(tiles) + len(chips))
    pick_copies = [
        send(picks.at[device[0]], parts.at[k], pick_send.at[k], pick_recv.at[k], device)
        for k, device in enumerate(tiles)
    ]

    loads["x"].wait()
    loads["first"].wait()
    halves_ref[...] = dot(first_ref[...], x_ref[...]).astype(bf16)

    template = picks[tile].astype(f32)
    for k, copy in enumerate(pick_copies):
        copy.wait()
        template = template + parts[k].astype(f32)
    held[core, chip, tile] = template.astype(bf16)
    own = held.at[core, chip, tile]
    spread_copies = [
        send(own, own, spread_send.at[k], spread_recv.at[k], device)
        for k, device in enumerate(chips)
    ]

    def source(k):
        return lax.rem(chip + n_chip - k, n_chip)

    def gather(k):
        strip_ref = held.at[core, source(k), tile]
        return [
            send(strip_ref, strip_ref, gather_send.at[k, j], gather_recv.at[k, j], device)
            for j, device in enumerate(tiles)
        ]

    gathers = [gather(0)]

    loads["cos"].wait()
    loads["sin"].wait()
    sums = {}
    for which in range(2):
        side = core if which else 1 - core
        columns = pl.ds(pl.multiple_of(side * half, half), half)
        half_real, half_imag = halves_ref[:rows], halves_ref[rows:]
        cosine, sine = cos_ref[:, columns], sin_ref[:, columns]
        spec_real = dot(half_real, cosine) + dot(half_imag, sine)
        spec_imag = dot(half_imag, cosine) - dot(half_real, sine)
        real_ref[:, columns] = spec_real
        imag_ref[:, columns] = spec_imag
        power = spec_real * spec_real + spec_imag * spec_imag
        if which == 0:
            pow_ref[...] = power.astype(bf16)
            pair_copy = send(pow_ref, pair_ref, pair_send, pair_recv, partner)
        else:
            total_ref[core] = power
    for k in range(1, n_chip):
        spread_copies[k - 1].wait()
        gathers.append(gather(k))
    tile_contrast((off_ref[core, 0] - off_ref[core, 1]).astype(f32), con_ref)

    def across(s):
        up, down = strides[s], strides[-1 - s]
        other = [tile + d * (1 - 2 * lax.rem(tile // d, 2)) for d in (up, down)]
        return (other[0] * (1 - core) + other[1] * core, orient)

    def sum_step(s):
        sum_out[s] = total_ref[core].astype(bf16)
        return send(sum_out.at[s], sum_in.at[s], sum_send.at[s], sum_recv.at[s], across(s))

    pair_copy.wait()
    total_ref[core] = total_ref[core] + pair_ref[...].astype(f32)
    pending = [sum_step(0)]

    def sum_next():
        s = len(pending) - 1
        pending[s].wait()
        total_ref[core] = total_ref[core] + sum_in[s].astype(f32)
        if s + 1 < len(strides):
            pending.append(sum_step(s + 1))
        else:
            mine = total_ref.at[core]
            pending.append(send(mine, mine, done_send, done_recv, partner))

    batch = min(n_chip, 4)

    def spectra(which, place, at):
        images = held[which, place]
        images = jnp.concatenate([images[:, s].reshape(size, size) for s in range(steps)], axis=1)
        template_spectra(
            images, small_ref, table_ref, base_ref, power_ref, lambda n: steps * at + n
        )

    loads["small"].wait()
    loads["table"].wait()
    swaps = []
    for k in range(n_chip):
        for copy in gathers[k]:
            copy.wait()
        block = held.at[core, source(k)]
        swaps.append(send(block, block, swap_send.at[k], swap_recv.at[k], partner))
        if n_chip == batch:
            spectra(core, source(k), core * batch + source(k))
        if k % 2 == 1 and len(pending) <= len(strides):
            sum_next()
    while len(pending) <= len(strides):
        sum_next()
    for k in range(n_chip):
        swaps[k].wait()
        if n_chip == batch:
            spectra(1 - core, source(k), (1 - core) * batch + source(k))
    pending[-1].wait()
    tile_gains(
        n_tile * 2, total_ref, real_ref, imag_ref, con_ref, g_real, g_imag, g_energy
    )
    loads["back"].wait()
    loads["last"].wait()
    count = 2 * batch * steps
    rounds = n_chip // batch
    out_copies = []
    for turn in range(rounds):
        if n_chip != batch:
            def fill(i, carry):
                spectra(i // batch, turn * batch + lax.rem(i, batch), i)
                return carry

            lax.fori_loop(0, 2 * batch, fill, 0)

        def weigh(t, carry):
            energy(t, power_ref, g_energy, part_ref)
            return carry

        lax.fori_loop(0, count, weigh, 0)

        def visit(group, carry):
            for u in range(4):
                t = group * 4 + u
                column = pl.ds(pl.multiple_of(t * quarter, quarter), quarter)
                half_back(t, column, base_ref, back_ref, g_real, g_imag, mids)
            return carry

        lax.fori_loop(0, count // 4, visit, 0)
        scales = scales_of(part_ref, count)
        for k in range(valid // quarter):
            for n in range(count // 2):
                fresh = turn == 0 and n == 0
                statistics(k, n, fresh, scales[2 * n : 2 * n + 2], mids, last_ref, stat_ref.at[k])
            if turn == rounds - 1:
                found = finish((stat_ref[k, 0], stat_ref[k, 1], stat_ref[k, 2]), rounds * count)
                columns = slice(k * quarter, (k + 1) * quarter)
                for which in range(2):
                    out_ref[which, core, :, columns] = found[which].astype(bf16)
                    block = out_ref.at[which, core, :, columns]
                    sems = out_send.at[k, which], out_recv.at[k, which]
                    out_copies.append(send(block, block, *sems, partner))
    for copy in out_copies:
        copy.wait()


def body(n_tile, n_orient, micrograph_tiles, tile_offsets, library, orient_ids):
    tile_count, length = micrograph_tiles.shape[:2]
    slots, _, size, _ = library.shape
    steps = orient_ids.shape[1]
    n_chip = n_orient // 2
    assert tile_count == 2 and n_orient % 2 == 0 and n_tile & (n_tile - 1) == 0
    assert n_chip % min(n_chip, 4) == 0 and steps == 2
    half, quarter = length // 2, length // 4
    assert size == quarter and VALID % quarter == 0
    t = tables(length, size, VALID)
    rows = t["first"].shape[0] // 2
    names = ("first", "cos", "sin", "small", "base", "back", "last")
    count = 2 * min(n_chip, 4) * steps
    levels = (n_tile - 1).bit_length()
    strip = size // n_tile
    shape = jax.ShapeDtypeStruct
    vmem, dma = pltpu.VMEM, pltpu.SemaphoreType.DMA
    both = pl.pallas_call(
        functools.partial(search_kernel, n_tile, n_orient, VALID),
        out_shape=shape((2, 2, VALID, VALID), bf16),
        in_specs=[SMEM, SMEM] + [ANY] * 9,
        out_specs=VMEM,
        scratch_shapes=[
            vmem((length, length), bf16),
            vmem(library.shape, bf16),
            *[vmem(t[name].shape, bf16) for name in names],
            *[vmem((rows, length), f32)] * 3,
            vmem((2 * rows, length), bf16),
            vmem((rows, half), bf16),
            vmem((rows, half), bf16),
            vmem((levels, rows, half), bf16),
            vmem((levels, rows, half), bf16),
            vmem((2, rows, half), f32),
            vmem((n_tile, steps, strip, size), bf16),
            vmem((n_tile - 1, steps, strip, size), bf16),
            vmem((2, n_chip, n_tile, steps, strip, size), bf16),
            *[vmem((rows, length), bf16)] * 3,
            vmem((count, rows, 2 * length), bf16),
            vmem((count, rows, length), bf16),
            vmem((count, 8, quarter), f32),
            vmem((VALID // quarter, length, count * quarter), bf16),
            vmem((VALID // quarter, 3, VALID, quarter), f32),
            dma((9,)),
            dma((n_tile - 1,)),
            dma((n_tile - 1,)),
            dma((n_chip - 1,)),
            dma((n_chip - 1,)),
            dma((n_chip, n_tile - 1)),
            dma((n_chip, n_tile - 1)),
            dma((n_chip,)),
            dma((n_chip,)),
            dma, dma,
            dma((levels,)),
            dma((levels,)),
            dma, dma,
            dma((VALID // quarter, 2)),
            dma((VALID // quarter, 2)),
        ],
        compiler_params=pltpu.CompilerParams(
            collective_id=0, has_side_effects=True, vmem_limit_bytes=GRANT
        ),
    )(orient_ids, tile_offsets, micrograph_tiles, library, *[t[name] for name in names])
    return (both[0].astype(f32), both[1].astype(f32))


def solution(mesh):
    placed = (
        P("tile", None, None),
        P("tile", None),
        P("tile", "orient", None, None),
        P("orient", None),
    )
    return jax.shard_map(
        functools.partial(body, mesh.shape["tile"], mesh.shape["orient"]),
        mesh=mesh,
        in_specs=placed,
        out_specs=(P("tile", None, None), P("tile", None, None)),
        check_vma=False,
    )
```

time: 50.6 us -> 50.8 us (level)
  local copies, waits for them, and re-layouts: 0 us -> 10.6 us
  Pallas kernels: 46.9 us -> 37.5 us
  other arithmetic: 2.8 us -> 1.56 us
    unnamed x0 -> x22, local copies, waits for them, and re-layouts: none -> 10.6 us
    pallas_call x4 -> x1, Pallas kernels: 46.9 us -> 37.5 us  [body(): pl.pallas_call(functools.partial(search_kernel, n_tile, n_orient, VALID),...]
    convert_element_type x1, other arithmetic: 2.8 us -> 1.56 us  [body(): return (both[0].astype(f32), both[1].astype(f32))]
where the time goes in v1:
time: 50.8 us; the launch traced here: 50.3 us
  Pallas kernels  37.5 us (74%)
  local copies, waits for them, and re-layouts  10.6 us (21%)
  other arithmetic  1.56 us (3%)
  between operations  0.66 us (1%)
    pallas_call x1, Pallas kernels, body(): pl.pallas_call(functools.partial(search_kernel, n_tile, n_orient, VALID),...  37.5 us
    unnamed x22, local copies, waits for them, and re-layouts  10.6 us
    convert_element_type x1, other arithmetic, body(): return (both[0].astype(f32), both[1].astype(f32))  1.56 us

profile of v1, /device:TPU:0, one launch (start us, length us, event | category | flops | bytes accessed | tf_op | source)
XLA Modules:
  0.0 50.3 jit_solution(1026637581709337616)
XLA Ops:
  0.6 0.0 copy-start
  0.6 1.2 %copy-done = bf16[2,512,512]{2,1,0:T(8,128)(2,1)S(1)} copy-done((bf16[2,512,512]{2,1,0:T(8,128)(2,1)S(1)}, bf16[2,512,512]{2,1,0:T(8,128)(2,1)}, u32[]{:S(2)}) %copy-start) | copy-done | bytes 1048600
  1.9 0.0 copy-start.1
  1.9 1.1 %copy-done.1 = bf16[544,512]{1,0:T(8,128)(2,1)S(1)} copy-done((bf16[544,512]{1,0:T(8,128)(2,1)S(1)}, bf16[544,512]{1,0:T(8,128)(2,1)}, u32[]{:S(2)}) %copy-start.1) | copy-done | bytes 557080
  2.9 0.0 copy-start.2
  2.9 1.0 %copy-done.2 = bf16[4,256,256]{2,1,0:T(8,128)(2,1)S(1)} copy-done((bf16[4,256,256]{2,1,0:T(8,128)(2,1)S(1)}, bf16[4,256,256]{2,1,0:T(8,128)(2,1)}, u32[]{:S(2)}) %copy-start.2) | copy-done | bytes 524312
  4.0 0.0 copy-start.3
  4.0 1.0 %copy-done.3 = bf16[256,1024]{1,0:T(8,128)(2,1)S(1)} copy-done((bf16[256,1024]{1,0:T(8,128)(2,1)S(1)}, bf16[256,1024]{1,0:T(8,128)(2,1)}, u32[]{:S(2)}) %copy-start.3) | copy-done | bytes 524312
  5.0 0.0 copy-start.4
  5.0 1.0 %copy-done.4 = bf16[512,512]{1,0:T(8,128)(2,1)S(1)} copy-done((bf16[512,512]{1,0:T(8,128)(2,1)S(1)}, bf16[512,512]{1,0:T(8,128)(2,1)}, u32[]{:S(2)}) %copy-start.4) | copy-done | bytes 524312
  6.0 0.0 copy-start.5
  6.0 1.0 %copy-done.5 = bf16[512,512]{1,0:T(8,128)(2,1)S(1)} copy-done((bf16[512,512]{1,0:T(8,128)(2,1)S(1)}, bf16[512,512]{1,0:T(8,128)(2,1)}, u32[]{:S(2)}) %copy-start.5) | copy-done | bytes 524312
  7.1 0.0 copy-start.6
  7.1 0.9 %copy-done.6 = bf16[8,1,128,128]{3,2,1,0:T(8,128)(2,1)S(1)} copy-done((bf16[8,1,128,128]{3,2,1,0:T(8,128)(2,1)S(1)}, bf16[8,1,128,128]{3,2,1,0:T(8,128)(2,1)}, u32[]{:S(2)}) %copy-start.6) | copy-done | bytes 262168
  8.0 0.0 copy-start.7
  8.0 0.9 %copy-done.7 = bf16[2,256,256]{2,1,0:T(8,128)(2,1)S(1)} copy-done((bf16[2,256,256]{2,1,0:T(8,128)(2,1)S(1)}, bf16[2,256,256]{2,1,0:T(8,128)(2,1)}, u32[]{:S(2)}) %copy-start.7) | copy-done | bytes 262168
  9.0 0.0 copy-start.8
  9.0 0.9 %copy-done.8 = bf16[544,128]{1,0:T(8,128)(2,1)S(1)} copy-done((bf16[544,128]{1,0:T(8,128)(2,1)S(1)}, bf16[544,128]{1,0:T(8,128)(2,1)}, u32[]{:S(2)}) %copy-start.8) | copy-done | bytes 139288
  9.9 0.0 copy-start.9
  9.9 0.7 %copy-done.9 = s32[2,2]{1,0:T(2,128)S(1)} copy-done((s32[2,2]{1,0:T(2,128)S(1)}, s32[2,2]{1,0:T(2,128)}, u32[]{:S(2)}) %copy-start.9) | copy-done | bytes 40
  10.6 0.0 copy-start.10
  10.6 0.7 %copy-done.10 = s32[1,2]{1,0:T(1,128)S(1)} copy-done((s32[1,2]{1,0:T(1,128)S(1)}, s32[1,2]{1,0:T(1,128)}, u32[]{:S(2)}) %copy-start.10) | copy-done | bytes 32
  11.2 37.5 %shard_map.122 = bf16[2,2,384,384]{3,2,1,0:T(8,128)(2,1)S(1)} custom-call(s32[1,2]{1,0:T(1,128)S(1)} %copy-done.10, s32[2,2]{1,0:T(2,128)S(1)} %copy-done.9, bf16[2,512,512]{2,1,0:T(8,128)(2,1)S(1)} %copy-done, bf16[8,1,128,128]{3,2,1,0:T(8,128)(2,1)S(1)} %copy-done.6, bf16[544,512]{1,0:T(8,128)(2,1)S(1)} %copy-done.1, bf16[512,512]{1,0:T(8,128)(2,1)S(1)} %copy-done.5, ...), custom_call_target="tpu_custom_call" | custom-call | tf_op jit(solution)/shard_map/pallas_call | solution.py:460
  48.7 1.6 %bitcast_convert_fusion = (f32[2,384,384]{2,1,0:T(8,128)}, f32[2,384,384]{2,1,0:T(8,128)}) fusion(bf16[2,2,384,384]{3,2,1,0:T(8,128)(2,1)S(1)} %shard_map.122), kind=kLoop, calls=%fused_computation | loop fusion | flops 589824 | bytes 3538944 | tf_op jit(solution)/shard_map/convert_element_type | solution.py:505
Async XLA Ops:
  0.6 1.2 %copy-start = (bf16[2,512,512]{2,1,0:T(8,128)(2,1)S(1)}, bf16[2,512,512]{2,1,0:T(8,128)(2,1)}, u32[]{:S(2)}) copy-start(bf16[2,512,512]{2,1,0:T(8,128)(2,1)} %x_hbm.1) | copy-start | bytes 3145732
  1.9 1.1 %copy-start.1 = (bf16[544,512]{1,0:T(8,128)(2,1)S(1)}, bf16[544,512]{1,0:T(8,128)(2,1)}, u32[]{:S(2)}) copy-start(bf16[544,512]{1,0:T(8,128)(2,1)} %constant.14.clone.first_hbm) | copy-start | bytes 1671172
  2.9 1.0 %copy-start.2 = (bf16[4,256,256]{2,1,0:T(8,128)(2,1)S(1)}, bf16[4,256,256]{2,1,0:T(8,128)(2,1)}, u32[]{:S(2)}) copy-start(bf16[4,256,256]{2,1,0:T(8,128)(2,1)} %constant.19.clone.back_hbm) | copy-start | bytes 1572868
  4.0 1.0 %copy-start.3 = (bf16[256,1024]{1,0:T(8,128)(2,1)S(1)}, bf16[256,1024]{1,0:T(8,128)(2,1)}, u32[]{:S(2)}) copy-start(bf16[256,1024]{1,0:T(8,128)(2,1)} %constant.18.clone.table_hbm) | copy-start | bytes 1572868
  5.0 1.0 %copy-start.4 = (bf16[512,512]{1,0:T(8,128)(2,1)S(1)}, bf16[512,512]{1,0:T(8,128)(2,1)}, u32[]{:S(2)}) copy-start(bf16[512,512]{1,0:T(8,128)(2,1)} %constant.16.clone.sin_hbm) | copy-start | bytes 1572868
  6.0 1.0 %copy-start.5 = (bf16[512,512]{1,0:T(8,128)(2,1)S(1)}, bf16[512,512]{1,0:T(8,128)(2,1)}, u32[]{:S(2)}) copy-start(bf16[512,512]{1,0:T(8,128)(2,1)} %constant.15.clone.cos_hbm) | copy-start | bytes 1572868
  7.1 0.9 %copy-start.6 = (bf16[8,1,128,128]{3,2,1,0:T(8,128)(2,1)S(1)}, bf16[8,1,128,128]{3,2,1,0:T(8,128)(2,1)}, u32[]{:S(2)}) copy-start(bf16[8,1,128,128]{3,2,1,0:T(8,128)(2,1)} %lib_hbm.1) | copy-start | bytes 786436
  8.0 0.9 %copy-start.7 = (bf16[2,256,256]{2,1,0:T(8,128)(2,1)S(1)}, bf16[2,256,256]{2,1,0:T(8,128)(2,1)}, u32[]{:S(2)}) copy-start(bf16[2,256,256]{2,1,0:T(8,128)(2,1)} %constant.20.clone.last_hbm) | copy-start | bytes 786436
  9.0 0.9 %copy-start.8 = (bf16[544,128]{1,0:T(8,128)(2,1)S(1)}, bf16[544,128]{1,0:T(8,128)(2,1)}, u32[]{:S(2)}) copy-start(bf16[544,128]{1,0:T(8,128)(2,1)} %constant.17.clone.small_hbm) | copy-start | bytes 417796
  9.9 0.7 %copy-start.9 = (s32[2,2]{1,0:T(2,128)S(1)}, s32[2,2]{1,0:T(2,128)}, u32[]{:S(2)}) copy-start(s32[2,2]{1,0:T(2,128)} %off_ref.1) | copy-start | bytes 52
  10.6 0.7 %copy-start.10 = (s32[1,2]{1,0:T(1,128)S(1)}, s32[1,2]{1,0:T(1,128)}, u32[]{:S(2)}) copy-start(s32[1,2]{1,0:T(1,128)} %ids_ref.1) | copy-start | bytes 28

commit v2 on v1

--- a/solution.py
+++ b/solution.py
@@ -17,8 +17,7 @@
 f32, bf16 = jnp.float32, jnp.bfloat16
 MESH = pl.DeviceIdType.MESH
 VMEM = pl.BlockSpec(memory_space=pltpu.VMEM)
-SMEM = pl.BlockSpec(memory_space=pltpu.SMEM)
-ANY = pl.BlockSpec(memory_space=pl.ANY)
+HBM = pl.BlockSpec(memory_space=pltpu.HBM)
 GRANT = 46 * 1024 * 1024
 
 
@@ -98,8 +97,8 @@
     return jnp.where(row > half, 0.0, jnp.where(single, 1.0, 2.0)).astype(f32)
 
 
-def tile_contrast(tilt, con_ref):
-    rows, length = con_ref.shape
+def tile_contrast(tilt, real_ref, imag_ref, seen_real, seen_imag, seen_energy):
+    rows, length = real_ref.shape
     half, quarter = length // 2, length // 4
     row, b_index = row_index(rows, half)
     b_index = jnp.where(row > half, 0, b_index).astype(f32) / length
@@ -110,10 +109,15 @@
     defocus = DEFOCUS_BASE + DEFOCUS_TILT * tilt
     shift = math.asin(AMPLITUDE) / (2.0 * math.pi)
     contrast = -sine_of_turns(s2 * (0.5 * defocus) + shift)
-    con_ref[...] = jnp.where(s2 > 0.0, contrast, 0.0)
-
-
-def template_spectra(images, small_ref, table_ref, base_ref, power_ref, place):
+    contrast = jnp.where(s2 > 0.0, contrast, 0.0)
+    seen_real[...] = (real_ref[...] * contrast).astype(bf16)
+    seen_imag[...] = (imag_ref[...] * contrast).astype(bf16)
+    seen_energy[...] = (contrast * contrast * (row_weight(rows, half) / (length * length))).astype(bf16)
+
+
+def template_spectra(
+    images, small_ref, table_ref, seen_real, seen_imag, seen_energy, base_ref, power_ref, place
+):
     rows = small_ref.shape[0] // 2
     size = images.shape[0]
     half = table_ref.shape[1] // 4
@@ -123,32 +127,29 @@
         joined = jnp.concatenate([halves[:rows, columns], halves[rows:, columns]], axis=1)
         for side in range(2):
             at = 2 * side * half
-            real = dot(joined, table_ref[:, at : at + half])
-            imag = dot(joined, table_ref[:, at + half : at + 2 * half])
-            base_ref[place(n), :, at : at + half] = real.astype(bf16)
-            base_ref[place(n), :, at + half : at + 2 * half] = imag.astype(bf16)
-            power_ref[place(n), :, side * half : (side + 1) * half] = (real * real + imag * imag).astype(bf16)
-
-
-def tile_gains(tiles, total_ref, real_ref, imag_ref, con_ref, g_real, g_imag, g_energy):
-    rows, length = real_ref.shape
+            columns = slice(side * half, (side + 1) * half)
+            real = dot(joined, table_ref[:, at : at + half]).astype(bf16)
+            imag = dot(joined, table_ref[:, at + half : at + 2 * half]).astype(bf16)
+            left, right = seen_real[:, columns], seen_imag[:, columns]
+            base_ref[place(n), :, at : at + half] = left * real + right * imag
+            base_ref[place(n), :, at + half : at + 2 * half] = right * real - left * imag
+            power_ref[place(n), :, columns] = (real * real + imag * imag) * seen_energy[:, columns]
+
+
+def tile_gains(tiles, total_ref, gain_ref):
+    rows, length = gain_ref.shape
     half = length // 2
     weight = row_weight(rows, half)
     mean = (jnp.sum(total_ref[0] * weight) + jnp.sum(total_ref[1] * weight)) / tiles
     floor = FLOOR_SHARE * (mean / (length * length))
     for side in range(2):
         columns = slice(side * half, (side + 1) * half)
-        whiten2 = 1.0 / jnp.maximum(total_ref[side] / tiles, floor)
-        contrast = con_ref[:, columns]
-        gain = contrast * whiten2
-        g_real[:, columns] = (real_ref[:, columns] * gain).astype(bf16)
-        g_imag[:, columns] = (imag_ref[:, columns] * gain).astype(bf16)
-        g_energy[:, columns] = (contrast * gain * (weight / (length * length))).astype(bf16)
-
-
-def energy(t, power_ref, g_energy, part_ref):
-    rows, length = g_energy.shape
-    share = power_ref[t] * g_energy[...]
+        gain_ref[:, columns] = (1.0 / jnp.maximum(total_ref[side] / tiles, floor)).astype(bf16)
+
+
+def energy(t, power_ref, gain_ref, part_ref):
+    rows, length = gain_ref.shape
+    share = power_ref[t] * gain_ref[...]
     share = share[:, : length // 2] + share[:, length // 2 :]
     total = None
     for row in range(0, rows, 16):
@@ -158,19 +159,17 @@
     part_ref[t] = total[:, : length // 4] + total[:, length // 4 :]
 
 
-def half_back(t, column, base_ref, back_ref, g_real, g_imag, mids):
-    rows, length = g_real.shape
+def half_back(t, column, base_ref, back_ref, gain_ref, mids):
+    rows, length = gain_ref.shape
     quarter = length // 4
     half = 2 * quarter
     found = []
     for side in range(2):
         columns = slice(side * half, (side + 1) * half)
         at = 2 * side * half
-        base_real = base_ref[t, :, at : at + half]
-        base_imag = base_ref[t, :, at + half : at + 2 * half]
-        gain_real, gain_imag = g_real[:, columns], g_imag[:, columns]
-        prod_real = gain_real * base_real + gain_imag * base_imag
-        prod_imag = gain_imag * base_real - gain_real * base_imag
+        gain = gain_ref[:, columns]
+        prod_real = base_ref[t, :, at : at + half] * gain
+        prod_imag = base_ref[t, :, at + half : at + 2 * half] * gain
         for q in range(2):
             part = slice(q * quarter, (q + 1) * quarter)
             joined = jnp.concatenate([prod_real[:, part], prod_imag[:, part]], axis=1)
@@ -223,14 +222,23 @@
     return peak, (peak - mean) * lax.rsqrt(variance + 1e-06)
 
 
+def flip(index, bits):
+    at = 1
+    while at <= bits:
+        if bits & at:
+            index = index + at * (1 - 2 * lax.rem(index // at, 2))
+        at *= 2
+    return index
+
+
 def search_kernel(
     n_tile, n_orient, valid,
-    ids_ref, off_ref, x_hbm, lib_hbm, first_hbm, cos_hbm, sin_hbm, small_hbm, table_hbm, back_hbm,
+    ids_hbm, off_hbm, x_hbm, lib_hbm, first_hbm, cos_hbm, sin_hbm, small_hbm, table_hbm, back_hbm,
     last_hbm, out_ref,
-    x_ref, lib_ref, first_ref, cos_ref, sin_ref, small_ref, table_ref, back_ref, last_ref,
-    real_ref, imag_ref, con_ref, halves_ref, pow_ref, pair_ref, sum_out, sum_in, total_ref,
-    picks, parts, held, g_real, g_imag, g_energy, base_ref, power_ref, part_ref, mids, stat_ref,
-    local_sem, pick_send, pick_recv, spread_send, spread_recv, gather_send, gather_recv,
+    ids_ref, off_ref, x_ref, lib_ref, first_ref, cos_ref, sin_ref, small_ref, table_ref, back_ref, last_ref,
+    real_ref, imag_ref, halves_ref, pow_ref, pair_ref, sum_out, sum_in, total_ref, picks, parts,
+    held, seen_real, seen_imag, seen_energy, gain_ref, base_ref, power_ref, part_ref, mids, stat_ref,
+    local_sem, pick_send, pick_recv, spread_send, spread_recv,
     swap_send, swap_recv, pair_send, pair_recv, sum_send, sum_recv, done_send, done_recv,
     out_send, out_recv,
 ):
@@ -239,14 +247,13 @@
     core = lax.rem(orient, 2)
     chip = orient // 2
     n_chip = n_orient // 2
-    steps, size = picks.shape[1], picks.shape[3]
+    steps, size = picks.shape[0], picks.shape[1]
     slots = lib_ref.shape[0]
     rows, length = real_ref.shape
     half, quarter = length // 2, length // 4
     partner = (tile, chip * 2 + 1 - core)
-    tiles = [(lax.rem(tile + k, n_tile), orient) for k in range(1, n_tile)]
-    chips = [(tile, lax.rem(chip + k, n_chip) * 2 + core) for k in range(1, n_chip)]
-    strides = [1 << s for s in range((n_tile - 1).bit_length())]
+    tiles = [(flip(tile, k), orient) for k in range(1, n_tile)]
+    chips = [(tile, flip(chip, k) * 2 + core) for k in range(1, n_chip)]
 
     def local(at, src, dst):
         copy = pltpu.make_async_copy(src, dst, local_sem.at[at])
@@ -254,6 +261,8 @@
         return copy
 
     loads = dict(
+        ids=local(9, ids_hbm, ids_ref),
+        off=local(10, off_hbm, off_ref),
         lib=local(0, lib_hbm, lib_ref),
         x=local(1, x_hbm.at[core], x_ref),
         first=local(2, first_hbm, first_ref),
@@ -276,52 +285,25 @@
         copy.start()
         return copy
 
-    strip = size // n_tile
+    loads["ids"].wait()
     loads["lib"].wait()
     for step in range(steps):
         chosen = ids_ref[0, step]
         owner = chosen // slots
         picked = lib_ref[chosen - owner * slots, 0]
         keep = jnp.where(owner == tile, 1.0, 0.0).astype(f32)
-        picked = jnp.where(keep > 0.0, picked.astype(f32), 0.0).astype(bf16)
-        for q in range(n_tile):
-            picks[q, step] = picked[q * strip : (q + 1) * strip]
-    pl.semaphore_wait(barrier, 1 + len(tiles) + len(chips))
-    pick_copies = [
-        send(picks.at[device[0]], parts.at[k], pick_send.at[k], pick_recv.at[k], device)
-        for k, device in enumerate(tiles)
-    ]
-
+        picks[step] = jnp.where(keep > 0.0, picked.astype(f32), 0.0).astype(bf16)
     loads["x"].wait()
     loads["first"].wait()
     halves_ref[...] = dot(first_ref[...], x_ref[...]).astype(bf16)
 
-    template = picks[tile].astype(f32)
-    for k, copy in enumerate(pick_copies):
-        copy.wait()
-        template = template + parts[k].astype(f32)
-    held[core, chip, tile] = template.astype(bf16)
-    own = held.at[core, chip, tile]
-    spread_copies = [
-        send(own, own, spread_send.at[k], spread_recv.at[k], device)
-        for k, device in enumerate(chips)
+    pl.semaphore_wait(barrier, 1 + len(tiles) + len(chips))
+    pick_copies = [
+        send(picks, parts.at[k], pick_send.at[k], pick_recv.at[k], device)
+        for k, device in enumerate(tiles)
     ]
-
-    def source(k):
-        return lax.rem(chip + n_chip - k, n_chip)
-
-    def gather(k):
-        strip_ref = held.at[core, source(k), tile]
-        return [
-            send(strip_ref, strip_ref, gather_send.at[k, j], gather_recv.at[k, j], device)
-            for j, device in enumerate(tiles)
-        ]
-
-    gathers = [gather(0)]
-
     loads["cos"].wait()
     loads["sin"].wait()
-    sums = {}
     for which in range(2):
         side = core if which else 1 - core
         columns = pl.ds(pl.multiple_of(side * half, half), half)
@@ -337,65 +319,67 @@
             pair_copy = send(pow_ref, pair_ref, pair_send, pair_recv, partner)
         else:
             total_ref[core] = power
+    pair_copy.wait()
+    sum_out[...] = (total_ref[core] + pair_ref[...].astype(f32)).astype(bf16)
+    sum_copies = [
+        send(sum_out, sum_in.at[k], sum_send.at[k], sum_recv.at[k], device)
+        for k, device in enumerate(tiles)
+    ]
+
+    def swap(k):
+        block = held.at[core, flip(chip, k)]
+        return send(block, block, swap_send.at[k], swap_recv.at[k], partner)
+
+    template = picks[...].astype(f32)
+    for k, copy in enumerate(pick_copies):
+        copy.wait()
+        template = template + parts[k].astype(f32)
+    held[core, chip] = template.astype(bf16)
+    own = held.at[core, chip]
+    spread_copies = [
+        send(own, own, spread_send.at[k], spread_recv.at[k], device)
+        for k, device in enumerate(chips)
+    ]
+    swaps = [swap(0)]
+    loads["off"].wait()
+    tilt = (off_ref[core, 0] - off_ref[core, 1]).astype(f32)
+    tile_contrast(tilt, real_ref, imag_ref, seen_real, seen_imag, seen_energy)
+
+    batch = min(n_chip, 4)
+
+    def spectra(which, place, at):
+        images = held[which, place]
+        images = jnp.concatenate([images[s] for s in range(steps)], axis=1)
+        template_spectra(
+            images, small_ref, table_ref, seen_real, seen_imag, seen_energy, base_ref, power_ref,
+            lambda n: steps * at + n,
+        )
+
+    def early(which, k):
+        if n_chip == batch:
+            spectra(which, flip(chip, k), which * batch + flip(chip, k))
+
+    loads["small"].wait()
+    loads["table"].wait()
+    early(core, 0)
+    swaps[0].wait()
+    early(1 - core, 0)
+    total = sum_out[...].astype(f32)
+    for k, copy in enumerate(sum_copies):
+        copy.wait()
+        total = total + sum_in[k].astype(f32)
+    total_ref[core] = total
+    mine = total_ref.at[core]
+    done_copy = send(mine, mine, done_send, done_recv, partner)
     for k in range(1, n_chip):
         spread_copies[k - 1].wait()
-        gathers.append(gather(k))
-    tile_contrast((off_ref[core, 0] - off_ref[core, 1]).astype(f32), con_ref)
-
-    def across(s):
-        up, down = strides[s], strides[-1 - s]
-        other = [tile + d * (1 - 2 * lax.rem(tile // d, 2)) for d in (up, down)]
-        return (other[0] * (1 - core) + other[1] * core, orient)
-
-    def sum_step(s):
-        sum_out[s] = total_ref[core].astype(bf16)
-        return send(sum_out.at[s], sum_in.at[s], sum_send.at[s], sum_recv.at[s], across(s))
-
-    pair_copy.wait()
-    total_ref[core] = total_ref[core] + pair_ref[...].astype(f32)
-    pending = [sum_step(0)]
-
-    def sum_next():
-        s = len(pending) - 1
-        pending[s].wait()
-        total_ref[core] = total_ref[core] + sum_in[s].astype(f32)
-        if s + 1 < len(strides):
-            pending.append(sum_step(s + 1))
-        else:
-            mine = total_ref.at[core]
-            pending.append(send(mine, mine, done_send, done_recv, partner))
-
-    batch = min(n_chip, 4)
-
-    def spectra(which, place, at):
-        images = held[which, place]
-        images = jnp.concatenate([images[:, s].reshape(size, size) for s in range(steps)], axis=1)
-        template_spectra(
-            images, small_ref, table_ref, base_ref, power_ref, lambda n: steps * at + n
-        )
-
-    loads["small"].wait()
-    loads["table"].wait()
-    swaps = []
-    for k in range(n_chip):
-        for copy in gathers[k]:
-            copy.wait()
-        block = held.at[core, source(k)]
-        swaps.append(send(block, block, swap_send.at[k], swap_recv.at[k], partner))
-        if n_chip == batch:
-            spectra(core, source(k), core * batch + source(k))
-        if k % 2 == 1 and len(pending) <= len(strides):
-            sum_next()
-    while len(pending) <= len(strides):
-        sum_next()
-    for k in range(n_chip):
+        swaps.append(swap(k))
+        early(core, k)
+    for k in range(1, n_chip):
         swaps[k].wait()
-        if n_chip == batch:
-            spectra(1 - core, source(k), (1 - core) * batch + source(k))
-    pending[-1].wait()
-    tile_gains(
-        n_tile * 2, total_ref, real_ref, imag_ref, con_ref, g_real, g_imag, g_energy
-    )
+        early(1 - core, k)
+    done_copy.wait()
+    tile_gains(n_tile * 2, total_ref, gain_ref)
     loads["back"].wait()
     loads["last"].wait()
     count = 2 * batch * steps
@@ -410,7 +394,7 @@
             lax.fori_loop(0, 2 * batch, fill, 0)
 
         def weigh(t, carry):
-            energy(t, power_ref, g_energy, part_ref)
+            energy(t, power_ref, gain_ref, part_ref)
             return carry
 
         lax.fori_loop(0, count, weigh, 0)
@@ -419,7 +403,7 @@
             for u in range(4):
                 t = group * 4 + u
                 column = pl.ds(pl.multiple_of(t * quarter, quarter), quarter)
-                half_back(t, column, base_ref, back_ref, g_real, g_imag, mids)
+                half_back(t, column, base_ref, back_ref, gain_ref, mids)
             return carry
 
         lax.fori_loop(0, count // 4, visit, 0)
@@ -445,7 +429,7 @@
     slots, _, size, _ = library.shape
     steps = orient_ids.shape[1]
     n_chip = n_orient // 2
-    assert tile_count == 2 and n_orient % 2 == 0 and n_tile & (n_tile - 1) == 0
+    assert tile_count == 2 and n_orient % 2 == 0 and n_tile & (n_tile - 1) == 0 and n_chip & (n_chip - 1) == 0
     assert n_chip % min(n_chip, 4) == 0 and steps == 2
     half, quarter = length // 2, length // 4
     assert size == quarter and VALID % quarter == 0
@@ -453,47 +437,44 @@
     rows = t["first"].shape[0] // 2
     names = ("first", "cos", "sin", "small", "base", "back", "last")
     count = 2 * min(n_chip, 4) * steps
-    levels = (n_tile - 1).bit_length()
-    strip = size // n_tile
     shape = jax.ShapeDtypeStruct
     vmem, dma = pltpu.VMEM, pltpu.SemaphoreType.DMA
+    operands = orient_ids, tile_offsets, micrograph_tiles, library, *[t[name] for name in names]
     both = pl.pallas_call(
         functools.partial(search_kernel, n_tile, n_orient, VALID),
         out_shape=shape((2, 2, VALID, VALID), bf16),
-        in_specs=[SMEM, SMEM] + [ANY] * 9,
+        in_specs=[HBM] * 11,
         out_specs=VMEM,
         scratch_shapes=[
+            pltpu.SMEM(orient_ids.shape, jnp.int32),
+            pltpu.SMEM(tile_offsets.shape, jnp.int32),
             vmem((length, length), bf16),
             vmem(library.shape, bf16),
             *[vmem(t[name].shape, bf16) for name in names],
-            *[vmem((rows, length), f32)] * 3,
+            *[vmem((rows, length), f32)] * 2,
             vmem((2 * rows, length), bf16),
-            vmem((rows, half), bf16),
-            vmem((rows, half), bf16),
-            vmem((levels, rows, half), bf16),
-            vmem((levels, rows, half), bf16),
+            *[vmem((rows, half), bf16)] * 3,
+            vmem((n_tile - 1, rows, half), bf16),
             vmem((2, rows, half), f32),
-            vmem((n_tile, steps, strip, size), bf16),
-            vmem((n_tile - 1, steps, strip, size), bf16),
-            vmem((2, n_chip, n_tile, steps, strip, size), bf16),
-            *[vmem((rows, length), bf16)] * 3,
+            vmem((steps, size, size), bf16),
+            vmem((n_tile - 1, steps, size, size), bf16),
+            vmem((2, n_chip, steps, size, size), bf16),
+            *[vmem((rows, length), bf16)] * 4,
             vmem((count, rows, 2 * length), bf16),
             vmem((count, rows, length), bf16),
             vmem((count, 8, quarter), f32),
             vmem((VALID // quarter, length, count * quarter), bf16),
             vmem((VALID // quarter, 3, VALID, quarter), f32),
-            dma((9,)),
+            dma((11,)),
             dma((n_tile - 1,)),
             dma((n_tile - 1,)),
             dma((n_chip - 1,)),
             dma((n_chip - 1,)),
-            dma((n_chip, n_tile - 1)),
-            dma((n_chip, n_tile - 1)),
             dma((n_chip,)),
             dma((n_chip,)),
             dma, dma,
-            dma((levels,)),
-            dma((levels,)),
+            dma((n_tile - 1,)),
+            dma((n_tile - 1,)),
             dma, dma,
             dma((VALID // quarter, 2)),
             dma((VALID // quarter, 2)),
@@ -501,7 +482,7 @@
         compiler_params=pltpu.CompilerParams(
             collective_id=0, has_side_effects=True, vmem_limit_bytes=GRANT
         ),
-    )(orient_ids, tile_offsets, micrograph_tiles, library, *[t[name] for name in names])
+    )(*[pltpu.with_memory_space_constraint(jnp.asarray(v), pltpu.HBM) for v in operands])
     return (both[0].astype(f32), both[1].astype(f32))
 
 

time: 50.8 us -> 34.1 us (0.67)
  local copies, waits for them, and re-layouts: 10.6 us -> 0 us
  Pallas kernels: 37.5 us -> 31.8 us
    unnamed x22 -> x0, local copies, waits for them, and re-layouts: 10.6 us -> none
    pallas_call x1, Pallas kernels: 37.5 us -> 31.8 us  [body(): pl.pallas_call(functools.partial(search_kernel, n_tile, n_orient, VALID),...]
where the time goes in v2:
time: 34.1 us; the launch traced here: 34 us
  Pallas kernels  31.8 us (93%)
  other arithmetic  1.56 us (5%)
  between operations  0.64 us (2%)
    pallas_call x1, Pallas kernels, body(): pl.pallas_call(functools.partial(search_kernel, n_tile, n_orient, VALID),...  31.8 us
    convert_element_type x1, other arithmetic, body(): return (both[0].astype(f32), both[1].astype(f32))  1.56 us

profile of v2, /device:TPU:0, one launch (start us, length us, event | category | flops | bytes accessed | tf_op | source)
XLA Modules:
  0.0 34.0 jit_solution(10677146471451441441)
XLA Ops:
  0.6 31.8 %shard_map.122 = bf16[2,2,384,384]{3,2,1,0:T(8,128)(2,1)S(1)} custom-call(s32[1,2]{1,0:T(1,128)} %ids_hbm.1, s32[2,2]{1,0:T(2,128)} %off_hbm.1, bf16[2,512,512]{2,1,0:T(8,128)(2,1)} %x_hbm.1, bf16[8,1,128,128]{3,2,1,0:T(8,128)(2,1)} %lib_hbm.1, bf16[544,512]{1,0:T(8,128)(2,1)} %constant.14.clone.first_hbm, bf16[512,512]{1,0:T(8,128)(2,1)} %constant.15.clone.cos_hbm, ...), custom_call_target="tpu_custom_call" | custom-call | tf_op jit(solution)/shard_map/pallas_call | solution.py:443
  32.4 1.6 %bitcast_convert_fusion = (f32[2,384,384]{2,1,0:T(8,128)}, f32[2,384,384]{2,1,0:T(8,128)}) fusion(bf16[2,2,384,384]{3,2,1,0:T(8,128)(2,1)S(1)} %shard_map.122), kind=kLoop, calls=%fused_computation | loop fusion | flops 589824 | bytes 3538944 | tf_op jit(solution)/shard_map/convert_element_type | solution.py:486

commit v3 on v2

--- a/solution.py
+++ b/solution.py
@@ -195,17 +195,21 @@
     return [lax.rsqrt(jnp.sum(part_ref[t]) + 1e-06) for t in range(count)]
 
 
-def statistics(k, n, fresh, scales, mids, last_ref, stat_ref):
+def statistics(k, first, fresh, scales, mids, last_ref, stat_ref):
     quarter = last_ref.shape[1] // 2
     half = 2 * quarter
-    columns = slice(n * half, (n + 1) * half)
+    columns = slice(first * quarter, (first + len(scales)) * quarter)
     even = dot(last_ref[0], mids[k, :half, columns])
     odd = dot(last_ref[1], mids[k, half:, columns])
-    one, two = scales
-    for rows, (e, o) in ((slice(0, half), (even, odd)), (slice(half, half + quarter), (even[:quarter], -odd[:quarter]))):
-        left = (e[:, :quarter] + o[:, :quarter]) * one
-        right = (e[:, quarter:] + o[:, quarter:]) * two
-        top, add, square = jnp.maximum(left, right), left + right, left * left + right * right
+    for rows, sign in ((slice(0, half), 1), (slice(half, half + quarter), -1)):
+        top = add = square = None
+        for n, scale in enumerate(scales):
+            e = even[: rows.stop - rows.start, n * quarter : (n + 1) * quarter]
+            o = odd[: rows.stop - rows.start, n * quarter : (n + 1) * quarter]
+            score = (e + o if sign > 0 else e - o) * scale
+            top = score if n == 0 else jnp.maximum(top, score)
+            add = score if n == 0 else add + score
+            square = score * score if n == 0 else square + score * score
         if not fresh:
             top = jnp.maximum(stat_ref[0, rows], top)
             add = stat_ref[1, rows] + add
@@ -229,6 +233,15 @@
             index = index + at * (1 - 2 * lax.rem(index // at, 2))
         at *= 2
     return index
+
+
+def flip_by(index, bits, count):
+    flipped, at = 0, 1
+    while at < count:
+        one, other = lax.rem(index // at, 2), lax.rem(bits // at, 2)
+        flipped = flipped + at * (one + other - 2 * one * other)
+        at *= 2
+    return flipped
 
 
 def search_kernel(
@@ -268,10 +281,6 @@
         first=local(2, first_hbm, first_ref),
         cos=local(3, cos_hbm, cos_ref),
         sin=local(4, sin_hbm, sin_ref),
-        small=local(5, small_hbm, small_ref),
-        table=local(6, table_hbm, table_ref),
-        back=local(7, back_hbm, back_ref),
-        last=local(8, last_hbm, last_ref),
     )
     barrier = pltpu.get_barrier_semaphore()
     for device in [partner] + tiles + chips:
@@ -293,17 +302,23 @@
         picked = lib_ref[chosen - owner * slots, 0]
         keep = jnp.where(owner == tile, 1.0, 0.0).astype(f32)
         picks[step] = jnp.where(keep > 0.0, picked.astype(f32), 0.0).astype(bf16)
-    loads["x"].wait()
-    loads["first"].wait()
-    halves_ref[...] = dot(first_ref[...], x_ref[...]).astype(bf16)
-
     pl.semaphore_wait(barrier, 1 + len(tiles) + len(chips))
     pick_copies = [
         send(picks, parts.at[k], pick_send.at[k], pick_recv.at[k], device)
         for k, device in enumerate(tiles)
     ]
+    loads["x"].wait()
+    loads["first"].wait()
+    halves_ref[...] = dot(first_ref[...], x_ref[...]).astype(bf16)
+
     loads["cos"].wait()
     loads["sin"].wait()
+    loads.update(
+        small=local(5, small_hbm, small_ref),
+        table=local(6, table_hbm, table_ref),
+        back=local(7, back_hbm, back_ref),
+        last=local(8, last_hbm, last_ref),
+    )
     for which in range(2):
         side = core if which else 1 - core
         columns = pl.ds(pl.multiple_of(side * half, half), half)
@@ -319,12 +334,29 @@
             pair_copy = send(pow_ref, pair_ref, pair_send, pair_recv, partner)
         else:
             total_ref[core] = power
+    levels = sum_in.shape[0]
+    cut = (rows // 32) * 16
+    pieces = [pl.ds(0, cut), pl.ds(cut, rows - cut)]
+    sums = {}
+
+    def sum_step(s, piece):
+        up, down = flip(tile, 1 << s), flip(tile, 1 << (levels - 1 - s))
+        device = (up * (1 - core) + down * core, orient)
+        at = s, pieces[piece]
+        sum_out[at] = total_ref[core, pieces[piece]].astype(bf16)
+        sems = sum_send.at[s, piece], sum_recv.at[s, piece]
+        sums[s, piece] = send(sum_out.at[at], sum_in.at[at], *sems, device)
+
+    def sum_wait(s, piece):
+        sums[s, piece].wait()
+        at = core, pieces[piece]
+        total_ref[at] = total_ref[at] + sum_in[s, pieces[piece]].astype(f32)
+
     pair_copy.wait()
-    sum_out[...] = (total_ref[core] + pair_ref[...].astype(f32)).astype(bf16)
-    sum_copies = [
-        send(sum_out, sum_in.at[k], sum_send.at[k], sum_recv.at[k], device)
-        for k, device in enumerate(tiles)
-    ]
+    for piece in range(2):
+        at = core, pieces[piece]
+        total_ref[at] = total_ref[at] + pair_ref[pieces[piece]].astype(f32)
+        sum_step(0, piece)
 
     def swap(k):
         block = held.at[core, flip(chip, k)]
@@ -361,27 +393,56 @@
 
     loads["small"].wait()
     loads["table"].wait()
-    early(core, 0)
+    for s in range(1, levels):
+        for piece in range(2):
+            sum_wait(s - 1, piece)
+            sum_step(s, piece)
+            if s == 1 and piece == 0:
+                early(core, 0)
     swaps[0].wait()
     early(1 - core, 0)
-    total = sum_out[...].astype(f32)
-    for k, copy in enumerate(sum_copies):
-        copy.wait()
-        total = total + sum_in[k].astype(f32)
-    total_ref[core] = total
-    mine = total_ref.at[core]
-    done_copy = send(mine, mine, done_send, done_recv, partner)
-    for k in range(1, n_chip):
+    done_copies = []
+    for piece in range(2):
+        sum_wait(levels - 1, piece)
+        mine = total_ref.at[core, pieces[piece]]
+        done_copies.append(send(mine, mine, done_send.at[piece], done_recv.at[piece], partner))
+    ready = (n_chip + 1) // 2
+    for k in range(1, ready):
         spread_copies[k - 1].wait()
         swaps.append(swap(k))
         early(core, k)
-    for k in range(1, n_chip):
+    for copy in done_copies:
+        copy.wait()
+    tile_gains(n_tile * 2, total_ref, gain_ref)
+    for k in range(1, ready):
         swaps[k].wait()
         early(1 - core, k)
-    done_copy.wait()
-    tile_gains(n_tile * 2, total_ref, gain_ref)
     loads["back"].wait()
     loads["last"].wait()
+
+    def search(begin, end):
+        def visit(k, carry):
+            place = flip_by(chip, k, batch) if n_chip == batch else k
+            for which in range(2):
+                for step in range(steps):
+                    t = (which * batch + place) * steps + step
+                    column = pl.ds(pl.multiple_of(t * quarter, quarter), quarter)
+                    energy(t, power_ref, gain_ref, part_ref)
+                    half_back(t, column, base_ref, back_ref, gain_ref, mids)
+            return carry
+
+        lax.fori_loop(begin, end, visit, 0)
+
+    if n_chip == batch:
+        search(0, ready)
+    for k in range(ready, n_chip):
+        spread_copies[k - 1].wait()
+        swaps.append(swap(k))
+    for k in range(ready, n_chip):
+        early(core, k)
+    for k in range(ready, n_chip):
+        swaps[k].wait()
+        early(1 - core, k)
     count = 2 * batch * steps
     rounds = n_chip // batch
     out_copies = []
@@ -393,25 +454,12 @@
 
             lax.fori_loop(0, 2 * batch, fill, 0)
 
-        def weigh(t, carry):
-            energy(t, power_ref, gain_ref, part_ref)
-            return carry
-
-        lax.fori_loop(0, count, weigh, 0)
-
-        def visit(group, carry):
-            for u in range(4):
-                t = group * 4 + u
-                column = pl.ds(pl.multiple_of(t * quarter, quarter), quarter)
-                half_back(t, column, base_ref, back_ref, gain_ref, mids)
-            return carry
-
-        lax.fori_loop(0, count // 4, visit, 0)
+        search(ready if n_chip == batch else 0, batch)
         scales = scales_of(part_ref, count)
         for k in range(valid // quarter):
-            for n in range(count // 2):
+            for n in range(0, count, 2):
                 fresh = turn == 0 and n == 0
-                statistics(k, n, fresh, scales[2 * n : 2 * n + 2], mids, last_ref, stat_ref.at[k])
+                statistics(k, n, fresh, scales[n : n + 2], mids, last_ref, stat_ref.at[k])
             if turn == rounds - 1:
                 found = finish((stat_ref[k, 0], stat_ref[k, 1], stat_ref[k, 2]), rounds * count)
                 columns = slice(k * quarter, (k + 1) * quarter)
@@ -437,6 +485,7 @@
     rows = t["first"].shape[0] // 2
     names = ("first", "cos", "sin", "small", "base", "back", "last")
     count = 2 * min(n_chip, 4) * steps
+    levels = (n_tile - 1).bit_length()
     shape = jax.ShapeDtypeStruct
     vmem, dma = pltpu.VMEM, pltpu.SemaphoreType.DMA
     operands = orient_ids, tile_offsets, micrograph_tiles, library, *[t[name] for name in names]
@@ -453,8 +502,8 @@
             *[vmem(t[name].shape, bf16) for name in names],
             *[vmem((rows, length), f32)] * 2,
             vmem((2 * rows, length), bf16),
-            *[vmem((rows, half), bf16)] * 3,
-            vmem((n_tile - 1, rows, half), bf16),
+            *[vmem((rows, half), bf16)] * 2,
+            *[vmem((levels, rows, half), bf16)] * 2,
             vmem((2, rows, half), f32),
             vmem((steps, size, size), bf16),
             vmem((n_tile - 1, steps, size, size), bf16),
@@ -473,9 +522,10 @@
             dma((n_chip,)),
             dma((n_chip,)),
             dma, dma,
-            dma((n_tile - 1,)),
-            dma((n_tile - 1,)),
-            dma, dma,
+            dma((levels, 2)),
+            dma((levels, 2)),
+            dma((2,)),
+            dma((2,)),
             dma((VALID // quarter, 2)),
             dma((VALID // quarter, 2)),
         ],

time: 34.1 us -> 32.9 us (0.965)
  Pallas kernels: 31.8 us -> 30.5 us
    pallas_call x1, Pallas kernels: 31.8 us -> 30.5 us  [body(): pl.pallas_call(functools.partial(search_kernel, n_tile, n_orient, VALID),...]
where the time goes in v3:
time: 32.9 us; the launch traced here: 32.7 us
  Pallas kernels  30.5 us (93%)
  other arithmetic  1.56 us (5%)
  between operations  0.64 us (2%)
    pallas_call x1, Pallas kernels, body(): pl.pallas_call(functools.partial(search_kernel, n_tile, n_orient, VALID),...  30.5 us
    convert_element_type x1, other arithmetic, body(): return (both[0].astype(f32), both[1].astype(f32))  1.56 us

profile of v3, /device:TPU:0, one launch (start us, length us, event | category | flops | bytes accessed | tf_op | source)
XLA Modules:
  0.0 32.7 jit_solution(14881350915561709420)
XLA Ops:
  0.6 30.5 %shard_map.122 = bf16[2,2,384,384]{3,2,1,0:T(8,128)(2,1)S(1)} custom-call(s32[1,2]{1,0:T(1,128)} %ids_hbm.1, s32[2,2]{1,0:T(2,128)} %off_hbm.1, bf16[2,512,512]{2,1,0:T(8,128)(2,1)} %x_hbm.1, bf16[8,1,128,128]{3,2,1,0:T(8,128)(2,1)} %lib_hbm.1, bf16[544,512]{1,0:T(8,128)(2,1)} %constant.14.clone.first_hbm, bf16[512,512]{1,0:T(8,128)(2,1)} %constant.15.clone.cos_hbm, ...), custom_call_target="tpu_custom_call" | custom-call | tf_op jit(solution)/shard_map/pallas_call | solution.py:492
  31.2 1.6 %bitcast_convert_fusion = (f32[2,384,384]{2,1,0:T(8,128)}, f32[2,384,384]{2,1,0:T(8,128)}) fusion(bf16[2,2,384,384]{3,2,1,0:T(8,128)(2,1)S(1)} %shard_map.122), kind=kLoop, calls=%fused_computation | loop fusion | flops 589824 | bytes 3538944 | tf_op jit(solution)/shard_map/convert_element_type | solution.py:536

commit v4 on v3

--- a/solution.py
+++ b/solution.py
@@ -130,10 +130,13 @@
             columns = slice(side * half, (side + 1) * half)
             real = dot(joined, table_ref[:, at : at + half]).astype(bf16)
             imag = dot(joined, table_ref[:, at + half : at + 2 * half]).astype(bf16)
-            left, right = seen_real[:, columns], seen_imag[:, columns]
-            base_ref[place(n), :, at : at + half] = left * real + right * imag
-            base_ref[place(n), :, at + half : at + 2 * half] = right * real - left * imag
-            power_ref[place(n), :, columns] = (real * real + imag * imag) * seen_energy[:, columns]
+            power = real * real + imag * imag
+            for which in range(seen_real.shape[0]):
+                slot = place(which, n)
+                left, right = seen_real[which, :, columns], seen_imag[which, :, columns]
+                base_ref[slot, :, at : at + half] = left * real + right * imag
+                base_ref[slot, :, at + half : at + 2 * half] = right * real - left * imag
+                power_ref[slot, :, columns] = power * seen_energy[which, :, columns]
 
 
 def tile_gains(tiles, total_ref, gain_ref):
@@ -191,14 +194,14 @@
         mids[k, 3 * quarter : 4 * quarter, column] = mid_imag[quarter : 2 * quarter].astype(bf16)
 
 
-def scales_of(part_ref, count):
-    return [lax.rsqrt(jnp.sum(part_ref[t]) + 1e-06) for t in range(count)]
+def scale_of(part):
+    return lax.rsqrt(jnp.sum(part) + 1e-06)
 
 
 def statistics(k, first, fresh, scales, mids, last_ref, stat_ref):
     quarter = last_ref.shape[1] // 2
     half = 2 * quarter
-    columns = slice(first * quarter, (first + len(scales)) * quarter)
+    columns = pl.ds(pl.multiple_of(first * quarter, quarter), len(scales) * quarter)
     even = dot(last_ref[0], mids[k, :half, columns])
     odd = dot(last_ref[1], mids[k, half:, columns])
     for rows, sign in ((slice(0, half), 1), (slice(half, half + quarter), -1)):
@@ -249,10 +252,11 @@
     ids_hbm, off_hbm, x_hbm, lib_hbm, first_hbm, cos_hbm, sin_hbm, small_hbm, table_hbm, back_hbm,
     last_hbm, out_ref,
     ids_ref, off_ref, x_ref, lib_ref, first_ref, cos_ref, sin_ref, small_ref, table_ref, back_ref, last_ref,
-    real_ref, imag_ref, halves_ref, pow_ref, pair_ref, sum_out, sum_in, total_ref, picks, parts,
-    held, seen_real, seen_imag, seen_energy, gain_ref, base_ref, power_ref, part_ref, mids, stat_ref,
+    real_ref, imag_ref, halves_ref, sum_out, sum_in, total_ref, picks, parts, held, seen_real,
+    seen_imag, seen_energy, gain_ref, base_ref, power_ref, part_ref, mids, stat_ref, share_out,
+    share_in,
     local_sem, pick_send, pick_recv, spread_send, spread_recv,
-    swap_send, swap_recv, pair_send, pair_recv, sum_send, sum_recv, done_send, done_recv,
+    share_send, share_recv, sum_send, sum_recv, done_send, done_recv,
     out_send, out_recv,
 ):
     tile = lax.axis_index("tile")
@@ -262,7 +266,7 @@
     n_chip = n_orient // 2
     steps, size = picks.shape[0], picks.shape[1]
     slots = lib_ref.shape[0]
-    rows, length = real_ref.shape
+    tile_count, rows, length = real_ref.shape
     half, quarter = length // 2, length // 4
     partner = (tile, chip * 2 + 1 - core)
     tiles = [(flip(tile, k), orient) for k in range(1, n_tile)]
@@ -277,7 +281,7 @@
         ids=local(9, ids_hbm, ids_ref),
         off=local(10, off_hbm, off_ref),
         lib=local(0, lib_hbm, lib_ref),
-        x=local(1, x_hbm.at[core], x_ref),
+        x=local(1, x_hbm, x_ref),
         first=local(2, first_hbm, first_ref),
         cos=local(3, cos_hbm, cos_ref),
         sin=local(4, sin_hbm, sin_ref),
@@ -304,12 +308,14 @@
         picks[step] = jnp.where(keep > 0.0, picked.astype(f32), 0.0).astype(bf16)
     pl.semaphore_wait(barrier, 1 + len(tiles) + len(chips))
     pick_copies = [
-        send(picks, parts.at[k], pick_send.at[k], pick_recv.at[k], device)
+        send(picks.at[step], parts.at[step, k], pick_send.at[step, k], pick_recv.at[step, k], device)
+        for step in range(steps)
         for k, device in enumerate(tiles)
     ]
     loads["x"].wait()
     loads["first"].wait()
-    halves_ref[...] = dot(first_ref[...], x_ref[...]).astype(bf16)
+    for which in range(tile_count):
+        halves_ref[which] = dot(first_ref[...], x_ref[which]).astype(bf16)
 
     loads["cos"].wait()
     loads["sin"].wait()
@@ -319,21 +325,22 @@
         back=local(7, back_hbm, back_ref),
         last=local(8, last_hbm, last_ref),
     )
-    for which in range(2):
-        side = core if which else 1 - core
+
+    def spectrum(side):
         columns = pl.ds(pl.multiple_of(side * half, half), half)
-        half_real, half_imag = halves_ref[:rows], halves_ref[rows:]
         cosine, sine = cos_ref[:, columns], sin_ref[:, columns]
-        spec_real = dot(half_real, cosine) + dot(half_imag, sine)
-        spec_imag = dot(half_imag, cosine) - dot(half_real, sine)
-        real_ref[:, columns] = spec_real
-        imag_ref[:, columns] = spec_imag
-        power = spec_real * spec_real + spec_imag * spec_imag
-        if which == 0:
-            pow_ref[...] = power.astype(bf16)
-            pair_copy = send(pow_ref, pair_ref, pair_send, pair_recv, partner)
-        else:
-            total_ref[core] = power
+        power = None
+        for which in range(tile_count):
+            half_real, half_imag = halves_ref[which, :rows], halves_ref[which, rows:]
+            spec_real = dot(half_real, cosine) + dot(half_imag, sine)
+            spec_imag = dot(half_imag, cosine) - dot(half_real, sine)
+            real_ref[which, :, columns] = spec_real
+            imag_ref[which, :, columns] = spec_imag
+            share = spec_real * spec_real + spec_imag * spec_imag
+            power = share if power is None else power + share
+        return power
+
+    total_ref[core] = spectrum(core)
     levels = sum_in.shape[0]
     cut = (rows // 32) * 16
     pieces = [pl.ds(0, cut), pl.ds(cut, rows - cut)]
@@ -352,44 +359,42 @@
         at = core, pieces[piece]
         total_ref[at] = total_ref[at] + sum_in[s, pieces[piece]].astype(f32)
 
-    pair_copy.wait()
     for piece in range(2):
-        at = core, pieces[piece]
-        total_ref[at] = total_ref[at] + pair_ref[pieces[piece]].astype(f32)
         sum_step(0, piece)
-
-    def swap(k):
-        block = held.at[core, flip(chip, k)]
-        return send(block, block, swap_send.at[k], swap_recv.at[k], partner)
-
-    template = picks[...].astype(f32)
-    for k, copy in enumerate(pick_copies):
-        copy.wait()
-        template = template + parts[k].astype(f32)
-    held[core, chip] = template.astype(bf16)
-    own = held.at[core, chip]
-    spread_copies = [
-        send(own, own, spread_send.at[k], spread_recv.at[k], device)
-        for k, device in enumerate(chips)
-    ]
-    swaps = [swap(0)]
+    spectrum(1 - core)
+    spread_copies = []
+    for step in range(steps):
+        template = picks[step].astype(f32)
+        for k in range(len(tiles)):
+            pick_copies[step * len(tiles) + k].wait()
+            template = template + parts[step, k].astype(f32)
+        held[chip, step] = template.astype(bf16)
+        own = held.at[chip, step]
+        spread_copies.append([
+            send(own, own, spread_send.at[step, k], spread_recv.at[step, k], device)
+            for k, device in enumerate(chips)
+        ])
     loads["off"].wait()
-    tilt = (off_ref[core, 0] - off_ref[core, 1]).astype(f32)
-    tile_contrast(tilt, real_ref, imag_ref, seen_real, seen_imag, seen_energy)
+    for which in range(tile_count):
+        tilt = (off_ref[which, 0] - off_ref[which, 1]).astype(f32)
+        tile_contrast(
+            tilt, real_ref.at[which], imag_ref.at[which], seen_real.at[which],
+            seen_imag.at[which], seen_energy.at[which],
+        )
 
     batch = min(n_chip, 4)
 
-    def spectra(which, place, at):
-        images = held[which, place]
+    def spectra(place, at):
+        images = held[place]
         images = jnp.concatenate([images[s] for s in range(steps)], axis=1)
         template_spectra(
             images, small_ref, table_ref, seen_real, seen_imag, seen_energy, base_ref, power_ref,
-            lambda n: steps * at + n,
+            lambda which, n: (which * batch + at) * steps + n,
         )
 
-    def early(which, k):
+    def early(k):
         if n_chip == batch:
-            spectra(which, flip(chip, k), which * batch + flip(chip, k))
+            spectra(flip(chip, k), flip(chip, k))
 
     loads["small"].wait()
     loads["table"].wait()
@@ -398,27 +403,28 @@
             sum_wait(s - 1, piece)
             sum_step(s, piece)
             if s == 1 and piece == 0:
-                early(core, 0)
-    swaps[0].wait()
-    early(1 - core, 0)
+                early(0)
+
+    def arrive(k):
+        for step in range(steps):
+            spread_copies[step][k - 1].wait()
+        early(k)
+
+    near = (n_chip + 1) // 2
+    for k in range(1, near):
+        arrive(k)
     done_copies = []
     for piece in range(2):
         sum_wait(levels - 1, piece)
         mine = total_ref.at[core, pieces[piece]]
         done_copies.append(send(mine, mine, done_send.at[piece], done_recv.at[piece], partner))
-    ready = (n_chip + 1) // 2
-    for k in range(1, ready):
-        spread_copies[k - 1].wait()
-        swaps.append(swap(k))
-        early(core, k)
+    for k in range(near, n_chip):
+        arrive(k)
+    loads["back"].wait()
+    loads["last"].wait()
     for copy in done_copies:
         copy.wait()
-    tile_gains(n_tile * 2, total_ref, gain_ref)
-    for k in range(1, ready):
-        swaps[k].wait()
-        early(1 - core, k)
-    loads["back"].wait()
-    loads["last"].wait()
+    tile_gains(n_tile * tile_count, total_ref, gain_ref)
 
     def search(begin, end):
         def visit(k, carry):
@@ -433,40 +439,43 @@
 
         lax.fori_loop(begin, end, visit, 0)
 
-    if n_chip == batch:
-        search(0, ready)
-    for k in range(ready, n_chip):
-        spread_copies[k - 1].wait()
-        swaps.append(swap(k))
-    for k in range(ready, n_chip):
-        early(core, k)
-    for k in range(ready, n_chip):
-        swaps[k].wait()
-        early(1 - core, k)
-    count = 2 * batch * steps
+    own = batch * steps
     rounds = n_chip // batch
-    out_copies = []
+    blocks = valid // quarter
+    shares, out_copies = [], []
     for turn in range(rounds):
         if n_chip != batch:
             def fill(i, carry):
-                spectra(i // batch, turn * batch + lax.rem(i, batch), i)
+                spectra(turn * batch + i, i)
                 return carry
 
-            lax.fori_loop(0, 2 * batch, fill, 0)
-
-        search(ready if n_chip == batch else 0, batch)
-        scales = scales_of(part_ref, count)
-        for k in range(valid // quarter):
-            for n in range(0, count, 2):
-                fresh = turn == 0 and n == 0
-                statistics(k, n, fresh, scales[n : n + 2], mids, last_ref, stat_ref.at[k])
-            if turn == rounds - 1:
-                found = finish((stat_ref[k, 0], stat_ref[k, 1], stat_ref[k, 2]), rounds * count)
+            lax.fori_loop(0, batch, fill, 0)
+        search(0, batch)
+        for mine in range(2):
+            which = core if mine else 1 - core
+            scales = [scale_of(part_ref[which * own + n]) for n in range(own)]
+            for k in range(blocks):
+                stats = stat_ref.at[mine, k]
+                for n in range(0, own, 2):
+                    fresh = turn == 0 and n == 0
+                    statistics(k, which * own + n, fresh, scales[n : n + 2], mids, last_ref, stats)
+                if turn < rounds - 1:
+                    continue
+                if not mine:
+                    share_out[k] = stats[...].astype(bf16)
+                    sems = share_send.at[k], share_recv.at[k]
+                    shares.append(send(share_out.at[k], share_in.at[k], *sems, partner))
+                    continue
+                shares[k].wait()
+                other = share_in[k].astype(f32)
+                peak = jnp.maximum(stats[0], other[0])
+                joined = peak, stats[1] + other[1], stats[2] + other[2]
+                found = finish(joined, 2 * rounds * own)
                 columns = slice(k * quarter, (k + 1) * quarter)
-                for which in range(2):
-                    out_ref[which, core, :, columns] = found[which].astype(bf16)
-                    block = out_ref.at[which, core, :, columns]
-                    sems = out_send.at[k, which], out_recv.at[k, which]
+                for kind in range(2):
+                    out_ref[kind, core, :, columns] = found[kind].astype(bf16)
+                    block = out_ref.at[kind, core, :, columns]
+                    sems = out_send.at[k, kind], out_recv.at[k, kind]
                     out_copies.append(send(block, block, *sems, partner))
     for copy in out_copies:
         copy.wait()
@@ -484,8 +493,9 @@
     t = tables(length, size, VALID)
     rows = t["first"].shape[0] // 2
     names = ("first", "cos", "sin", "small", "base", "back", "last")
-    count = 2 * min(n_chip, 4) * steps
+    count = tile_count * min(n_chip, 4) * steps
     levels = (n_tile - 1).bit_length()
+    blocks = VALID // quarter
     shape = jax.ShapeDtypeStruct
     vmem, dma = pltpu.VMEM, pltpu.SemaphoreType.DMA
     operands = orient_ids, tile_offsets, micrograph_tiles, library, *[t[name] for name in names]
@@ -497,37 +507,31 @@
         scratch_shapes=[
             pltpu.SMEM(orient_ids.shape, jnp.int32),
             pltpu.SMEM(tile_offsets.shape, jnp.int32),
-            vmem((length, length), bf16),
+            vmem(micrograph_tiles.shape, bf16),
             vmem(library.shape, bf16),
             *[vmem(t[name].shape, bf16) for name in names],
-            *[vmem((rows, length), f32)] * 2,
-            vmem((2 * rows, length), bf16),
-            *[vmem((rows, half), bf16)] * 2,
+            *[vmem((tile_count, rows, length), f32)] * 2,
+            vmem((tile_count, 2 * rows, length), bf16),
             *[vmem((levels, rows, half), bf16)] * 2,
             vmem((2, rows, half), f32),
             vmem((steps, size, size), bf16),
-            vmem((n_tile - 1, steps, size, size), bf16),
-            vmem((2, n_chip, steps, size, size), bf16),
-            *[vmem((rows, length), bf16)] * 4,
+            vmem((steps, n_tile - 1, size, size), bf16),
+            vmem((n_chip, steps, size, size), bf16),
+            *[vmem((tile_count, rows, length), bf16)] * 3,
+            vmem((rows, length), bf16),
             vmem((count, rows, 2 * length), bf16),
             vmem((count, rows, length), bf16),
             vmem((count, 8, quarter), f32),
-            vmem((VALID // quarter, length, count * quarter), bf16),
-            vmem((VALID // quarter, 3, VALID, quarter), f32),
+            vmem((blocks, length, count * quarter), bf16),
+            vmem((2, blocks, 3, VALID, quarter), f32),
+            *[vmem((blocks, 3, VALID, quarter), bf16)] * 2,
             dma((11,)),
-            dma((n_tile - 1,)),
-            dma((n_tile - 1,)),
-            dma((n_chip - 1,)),
-            dma((n_chip - 1,)),
-            dma((n_chip,)),
-            dma((n_chip,)),
-            dma, dma,
-            dma((levels, 2)),
-            dma((levels, 2)),
-            dma((2,)),
-            dma((2,)),
-            dma((VALID // quarter, 2)),
-            dma((VALID // quarter, 2)),
+            *[dma((steps, n_tile - 1))] * 2,
+            *[dma((steps, n_chip - 1))] * 2,
+            *[dma((blocks,))] * 2,
+            *[dma((levels, 2))] * 2,
+            *[dma((2,))] * 2,
+            *[dma((blocks, 2))] * 2,
         ],
         compiler_params=pltpu.CompilerParams(
             collective_id=0, has_side_effects=True, vmem_limit_bytes=GRANT

time: 32.9 us -> 32.1 us (0.976)
  Pallas kernels: 30.5 us -> 29.7 us
    pallas_call x1, Pallas kernels: 30.5 us -> 29.7 us  [body(): pl.pallas_call(functools.partial(search_kernel, n_tile, n_orient, VALID),...]
where the time goes in v4:
time: 32.1 us; the launch traced here: 31.9 us
  Pallas kernels  29.7 us (93%)
  other arithmetic  1.56 us (5%)
  between operations  0.64 us (2%)
    pallas_call x1, Pallas kernels, body(): pl.pallas_call(functools.partial(search_kernel, n_tile, n_orient, VALID),...  29.7 us
    convert_element_type x1, other arithmetic, body(): return (both[0].astype(f32), both[1].astype(f32))  1.56 us

profile of v4, /device:TPU:0, one launch (start us, length us, event | category | flops | bytes accessed | tf_op | source)
XLA Modules:
  0.0 31.9 jit_solution(8607399230332526271)
XLA Ops:
  0.6 29.7 %shard_map.122 = bf16[2,2,384,384]{3,2,1,0:T(8,128)(2,1)S(1)} custom-call(s32[1,2]{1,0:T(1,128)} %ids_hbm.1, s32[2,2]{1,0:T(2,128)} %off_hbm.1, bf16[2,512,512]{2,1,0:T(8,128)(2,1)} %x_hbm.1, bf16[8,1,128,128]{3,2,1,0:T(8,128)(2,1)} %lib_hbm.1, bf16[544,512]{1,0:T(8,128)(2,1)} %constant.14.clone.first_hbm, bf16[512,512]{1,0:T(8,128)(2,1)} %constant.15.clone.cos_hbm, ...), custom_call_target="tpu_custom_call" | custom-call | tf_op jit(solution)/shard_map/pallas_call | solution.py:502
  30.4 1.6 %bitcast_convert_fusion = (f32[2,384,384]{2,1,0:T(8,128)}, f32[2,384,384]{2,1,0:T(8,128)}) fusion(bf16[2,2,384,384]{3,2,1,0:T(8,128)(2,1)S(1)} %shard_map.122), kind=kLoop, calls=%fused_computation | loop fusion | flops 589824 | bytes 3538944 | tf_op jit(solution)/shard_map/convert_element_type | solution.py:540

commit v5 on v4

--- a/solution.py
+++ b/solution.py
@@ -281,15 +281,16 @@
         ids=local(9, ids_hbm, ids_ref),
         off=local(10, off_hbm, off_ref),
         lib=local(0, lib_hbm, lib_ref),
+    )
+    barrier = pltpu.get_barrier_semaphore()
+    for device in [partner] + tiles + chips:
+        pl.semaphore_signal(barrier, inc=1, device_id=device, device_id_type=MESH)
+    loads.update(
         x=local(1, x_hbm, x_ref),
         first=local(2, first_hbm, first_ref),
         cos=local(3, cos_hbm, cos_ref),
         sin=local(4, sin_hbm, sin_ref),
     )
-    barrier = pltpu.get_barrier_semaphore()
-    for device in [partner] + tiles + chips:
-        pl.semaphore_signal(barrier, inc=1, device_id=device, device_id_type=MESH)
-
     def send(src, dst, send_sem, recv_sem, device):
         copy = pltpu.make_async_remote_copy(
             src_ref=src, dst_ref=dst, send_sem=send_sem, recv_sem=recv_sem,
@@ -362,6 +363,13 @@
     for piece in range(2):
         sum_step(0, piece)
     spectrum(1 - core)
+    loads["off"].wait()
+    for which in range(tile_count):
+        tilt = (off_ref[which, 0] - off_ref[which, 1]).astype(f32)
+        tile_contrast(
+            tilt, real_ref.at[which], imag_ref.at[which], seen_real.at[which],
+            seen_imag.at[which], seen_energy.at[which],
+        )
     spread_copies = []
     for step in range(steps):
         template = picks[step].astype(f32)
@@ -374,14 +382,6 @@
             send(own, own, spread_send.at[step, k], spread_recv.at[step, k], device)
             for k, device in enumerate(chips)
         ])
-    loads["off"].wait()
-    for which in range(tile_count):
-        tilt = (off_ref[which, 0] - off_ref[which, 1]).astype(f32)
-        tile_contrast(
-            tilt, real_ref.at[which], imag_ref.at[which], seen_real.at[which],
-            seen_imag.at[which], seen_energy.at[which],
-        )
-
     batch = min(n_chip, 4)
 
     def spectra(place, at):
@@ -398,12 +398,11 @@
 
     loads["small"].wait()
     loads["table"].wait()
+    early(0)
     for s in range(1, levels):
         for piece in range(2):
             sum_wait(s - 1, piece)
             sum_step(s, piece)
-            if s == 1 and piece == 0:
-                early(0)
 
     def arrive(k):
         for step in range(steps):
@@ -437,7 +436,7 @@
                     half_back(t, column, base_ref, back_ref, gain_ref, mids)
             return carry
 
-        lax.fori_loop(begin, end, visit, 0)
+        lax.fori_loop(begin, end, visit, 0, unroll=2)
 
     own = batch * steps
     rounds = n_chip // batch

time: 32.1 us -> 30.9 us (0.963)
  Pallas kernels: 29.7 us -> 28.6 us
    pallas_call x1, Pallas kernels: 29.7 us -> 28.6 us  [body(): pl.pallas_call(functools.partial(search_kernel, n_tile, n_orient, VALID),...]
where the time goes in v5:
time: 30.9 us; the launch traced here: 30.8 us
  Pallas kernels  28.6 us (93%)
  other arithmetic  1.56 us (5%)
  between operations  0.64 us (2%)
    pallas_call x1, Pallas kernels, body(): pl.pallas_call(functools.partial(search_kernel, n_tile, n_orient, VALID),...  28.6 us
    convert_element_type x1, other arithmetic, body(): return (both[0].astype(f32), both[1].astype(f32))  1.56 us

profile of v5, /device:TPU:0, one launch (start us, length us, event | category | flops | bytes accessed | tf_op | source)
XLA Modules:
  0.0 30.8 jit_solution(17634190965474484748)
XLA Ops:
  0.6 28.6 %shard_map.122 = bf16[2,2,384,384]{3,2,1,0:T(8,128)(2,1)S(1)} custom-call(s32[1,2]{1,0:T(1,128)} %ids_hbm.1, s32[2,2]{1,0:T(2,128)} %off_hbm.1, bf16[2,512,512]{2,1,0:T(8,128)(2,1)} %x_hbm.1, bf16[8,1,128,128]{3,2,1,0:T(8,128)(2,1)} %lib_hbm.1, bf16[544,512]{1,0:T(8,128)(2,1)} %constant.14.clone.first_hbm, bf16[512,512]{1,0:T(8,128)(2,1)} %constant.15.clone.cos_hbm, ...), custom_call_target="tpu_custom_call" | custom-call | tf_op jit(solution)/shard_map/pallas_call | solution.py:501
  29.2 1.6 %bitcast_convert_fusion = (f32[2,384,384]{2,1,0:T(8,128)}, f32[2,384,384]{2,1,0:T(8,128)}) fusion(bf16[2,2,384,384]{3,2,1,0:T(8,128)(2,1)S(1)} %shard_map.122), kind=kLoop, calls=%fused_computation | loop fusion | flops 589824 | bytes 3538944 | tf_op jit(solution)/shard_map/convert_element_type | solution.py:539

commit v6 on v5

--- a/solution.py
+++ b/solution.py
@@ -436,7 +436,7 @@
                     half_back(t, column, base_ref, back_ref, gain_ref, mids)
             return carry
 
-        lax.fori_loop(begin, end, visit, 0, unroll=2)
+        lax.fori_loop(begin, end, visit, 0, unroll=batch if n_chip == batch else 1)
 
     own = batch * steps
     rounds = n_chip // batch

time: 30.9 us -> 30.6 us (level)
  Pallas kernels: 28.6 us -> 28.2 us
    pallas_call x1, Pallas kernels: 28.6 us -> 28.2 us  [body(): pl.pallas_call(functools.partial(search_kernel, n_tile, n_orient, VALID),...]
where the time goes in v6:
time: 30.6 us; the launch traced here: 30.4 us
  Pallas kernels  28.2 us (92%)
  other arithmetic  1.56 us (5%)
  between operations  0.64 us (2%)
    pallas_call x1, Pallas kernels, body(): pl.pallas_call(functools.partial(search_kernel, n_tile, n_orient, VALID),...  28.2 us
    convert_element_type x1, other arithmetic, body(): return (both[0].astype(f32), both[1].astype(f32))  1.56 us

profile of v6, /device:TPU:0, one launch (start us, length us, event | category | flops | bytes accessed | tf_op | source)
XLA Modules:
  0.0 30.4 jit_solution(12627128291228189399)
XLA Ops:
  0.6 28.2 %shard_map.122 = bf16[2,2,384,384]{3,2,1,0:T(8,128)(2,1)S(1)} custom-call(s32[1,2]{1,0:T(1,128)} %ids_hbm.1, s32[2,2]{1,0:T(2,128)} %off_hbm.1, bf16[2,512,512]{2,1,0:T(8,128)(2,1)} %x_hbm.1, bf16[8,1,128,128]{3,2,1,0:T(8,128)(2,1)} %lib_hbm.1, bf16[544,512]{1,0:T(8,128)(2,1)} %constant.14.clone.first_hbm, bf16[512,512]{1,0:T(8,128)(2,1)} %constant.15.clone.cos_hbm, ...), custom_call_target="tpu_custom_call" | custom-call | tf_op jit(solution)/shard_map/pallas_call | solution.py:501
  28.9 1.6 %bitcast_convert_fusion = (f32[2,384,384]{2,1,0:T(8,128)}, f32[2,384,384]{2,1,0:T(8,128)}) fusion(bf16[2,2,384,384]{3,2,1,0:T(8,128)(2,1)S(1)} %shard_map.122), kind=kLoop, calls=%fused_computation | loop fusion | flops 589824 | bytes 3538944 | tf_op jit(solution)/shard_map/convert_element_type | solution.py:539
